TPU v7x, 32 devices: a whole 2x2x4 slice. The times are simulated.
32 devices in a mesh: segment: 4 (over y, x), gy: 8 (over z, core).
Axes of the slice: x: 2, y: 2, z: 4, core: 2. Of those that a mesh axis runs over, the one named last changes fastest.
Arguments:
- crops: bfloat16 [2, 32, 4, 32, 128], P(None, None, None, 'gy'), may hold values from -6 to 6
- cotangent: bfloat16 [2, 32, 4, 32, 128], P(None, None, None, 'gy'), may hold values from -0.59765625 to 0.59765625
- weights: bfloat16 [4, 2, 27, 32, 32], P('segment'), may hold values from -0.375 to 0.375
Outputs:
- features: bfloat16 [4, 2, 32, 4, 32, 128], P('segment', None, None, None, 'gy')
- weight_grads: float32 [4, 2, 27, 32, 32], P('segment')
- input_grads: float32 [4, 2, 32, 4, 32, 128], P('segment', None, None, None, 'gy')
All inputs are finite; a program needn't handle non-finite values.
Results may differ from a plain program's by a relative error of at most 0.025.
Values may be sent and summed in bfloat16 or wider, within the bound.
A program may use at most 128 MiB of HBM per device.

v0:
```python
import jax
import jax.numpy as jnp
from jax import lax
from jax.sharding import PartitionSpec as P


def extended(block, sides, width):
    for axis, dim in sides:
        count = lax.axis_size(axis)
        forward = [(i, i + 1) for i in range(count - 1)]
        backward = [(target, source) for source, target in forward]
        low = lax.ppermute(
            lax.slice_in_dim(block, block.shape[dim] - width, None, axis=dim), axis, forward
        )
        high = lax.ppermute(lax.slice_in_dim(block, 0, width, axis=dim), axis, backward)
        block = jnp.concatenate([low, block, high], axis=dim)
    return block


def from_partner(array, axis, bit):
    return lax.ppermute(array, axis, [(i, i ^ 1 << bit) for i in range(lax.axis_size(axis))])


def passed_along(value, axis, steps):
    count = lax.axis_size(axis)
    first, last = (max(0, -steps), min(count, count - steps))
    return lax.ppermute(value, axis, [(source, source + steps) for source in range(first, last)])


def slices_of(padded, plane_shift, row_count):
    planes = padded.shape[1] - 2
    across = padded.shape[3] - 2
    return jnp.stack(
        [
            padded[
                :,
                plane_shift : plane_shift + planes,
                row_shift : row_shift + row_count,
                side_shift : side_shift + across,
            ]
            for row_shift in range(3)
            for side_shift in range(3)
        ]
    )


def convolve(padded, kernel, row_count):
    result = None
    for plane_shift in range(3):
        contribution = jnp.einsum(
            "tczyx,tco->ozyx",
            slices_of(padded, plane_shift, row_count),
            kernel[9 * plane_shift : 9 * plane_shift + 9],
            preferred_element_type=jnp.float32,
        )
        result = contribution if result is None else result + contribution
    return result


def kernel_grads(padded, gradient, row_count):
    pieces = []
    for plane_shift in range(3):
        pieces.append(
            jnp.einsum(
                "tczyx,ozyx->tco",
                slices_of(padded, plane_shift, row_count),
                gradient,
                preferred_element_type=jnp.float32,
            )
        )
    return jnp.concatenate(pieces, 0)


def flipped(kernel):
    return jnp.transpose(jnp.flip(kernel, 0), (0, 2, 1))


def slope(preact):
    logistic = jax.nn.sigmoid(preact)
    return logistic * (1.0 + preact * (1.0 - logistic))


def side_pad(volume):
    return jnp.pad(volume, ((0, 0), (1, 1), (0, 0), (1, 1)))


def gradient_rows(volume):
    return side_pad(extended(volume, (("gy", 2),), 1))


def mirror_forward(volume):
    for bit_number in range(2):
        volume = from_partner(volume, "segment", bit_number)
    return volume


def mirror_backward(volume):
    for bit_number in range(2):
        volume = from_partner(volume, "segment", bit_number)
    return volume


def pick(buffer, slot_index):
    return lax.dynamic_index_in_dim(buffer, slot_index, 0, keepdims=False)


def place(buffer, value, slot_index, active):
    return lax.dynamic_update_index_in_dim(
        buffer, jnp.where(active, value, pick(buffer, slot_index)), slot_index, 0
    )


def local(crops, cotangent, weights):
    micro_count, channels, planes, row_count, across = crops.shape
    segment_index = lax.axis_index("segment")
    row_offset = lax.axis_index("gy") * row_count
    all_rows = lax.axis_size("gy") * row_count
    moments = micro_count + 3
    kernel_first = weights[0, 0]
    kernel_second = weights[0, 1]
    block = (channels, planes, row_count, across)
    empty_block = jnp.zeros(block, jnp.bfloat16)
    padded_shape = (micro_count, channels, planes + 2, row_count + 2, across + 2)
    input_store = jnp.zeros(padded_shape, jnp.bfloat16)
    hidden_store = jnp.zeros(padded_shape, jnp.bfloat16)
    first_store = jnp.zeros((micro_count,) + block, jnp.float32)
    second_store = jnp.zeros((micro_count,) + block, jnp.float32)
    feature_store = jnp.zeros((micro_count,) + block, jnp.bfloat16)
    skip_store = jnp.zeros((micro_count,) + block, jnp.bfloat16)
    from_before = empty_block
    for moment in range(moments):
        position = moment - segment_index
        active = (position >= 0) & (position < micro_count)
        slot_index = jnp.clip(position, 0, micro_count - 1)
        entering = jnp.where(segment_index == 0, pick(crops, slot_index), from_before)
        skip_rows = pick(skip_store, slot_index)
        merged = jnp.where(
            segment_index >= 2,
            (entering.astype(jnp.float32) + skip_rows.astype(jnp.float32)).astype(jnp.bfloat16),
            entering,
        )
        widened = side_pad(extended(merged, (("gy", 2),), 2))
        pre_wide = convolve(widened, kernel_first, row_count + 2)
        global_rows = row_offset - 1 + jnp.arange(row_count + 2)
        inside = ((global_rows >= 0) & (global_rows < all_rows))[None, None, :, None]
        hidden_pad = side_pad(jnp.where(inside, jax.nn.silu(pre_wide), 0.0).astype(jnp.bfloat16))
        input_pad = widened[:, :, 1:-1]
        pre_first = pre_wide[:, :, 1:-1]
        pre_second = convolve(hidden_pad, kernel_second, row_count)
        leaving = jax.nn.silu(pre_second).astype(jnp.bfloat16)
        input_store = place(input_store, input_pad, slot_index, active)
        hidden_store = place(hidden_store, hidden_pad, slot_index, active)
        first_store = place(first_store, pre_first, slot_index, active)
        second_store = place(second_store, pre_second, slot_index, active)
        feature_store = place(feature_store, leaving, slot_index, active)
        if moment + 1 < moments:
            arrived_position = moment - (3 - segment_index)
            arrived = (
                (arrived_position >= 0) & (arrived_position < micro_count) & (segment_index >= 2)
            )
            skip_store = place(
                skip_store,
                mirror_forward(entering),
                jnp.clip(arrived_position, 0, micro_count - 1),
                arrived,
            )
            from_before = passed_along(leaving, "segment", 1)
    flip_first = flipped(kernel_first)
    flip_second = flipped(kernel_second)
    grad_sum = jnp.zeros((2,) + kernel_first.shape, jnp.float32)
    grad_store = jnp.zeros((micro_count,) + block, jnp.bfloat16)
    input_grads = jnp.zeros((micro_count,) + block, jnp.float32)
    from_after = empty_block
    for moment in range(moments):
        position = moment - (3 - segment_index)
        active = (position >= 0) & (position < micro_count)
        slot_index = jnp.clip(position, 0, micro_count - 1)
        incoming = jnp.where(segment_index == 3, pick(cotangent, slot_index), from_after)
        second_delta = (
            incoming.astype(jnp.float32) * slope(pick(second_store, slot_index))
        ).astype(jnp.bfloat16)
        grad_second = kernel_grads(pick(hidden_store, slot_index), second_delta, row_count)
        hidden_delta = convolve(gradient_rows(second_delta), flip_second, row_count)
        first_delta = (hidden_delta * slope(pick(first_store, slot_index))).astype(jnp.bfloat16)
        grad_first = kernel_grads(pick(input_store, slot_index), first_delta, row_count)
        grad_sum = grad_sum + jnp.where(active, jnp.stack([grad_first, grad_second]), 0.0)
        delta = convolve(gradient_rows(first_delta), flip_first, row_count).astype(jnp.bfloat16)
        extra = pick(grad_store, slot_index)
        summed = delta.astype(jnp.float32) + extra.astype(jnp.float32)
        input_grads = place(input_grads, summed, slot_index, active)
        passing = jnp.where(segment_index == 1, summed.astype(jnp.bfloat16), delta)
        if moment + 1 < moments:
            arrived_position = moment - segment_index
            arrived = (
                (arrived_position >= 0) & (arrived_position < micro_count) & (segment_index <= 1)
            )
            grad_store = place(
                grad_store,
                mirror_backward(delta),
                jnp.clip(arrived_position, 0, micro_count - 1),
                arrived,
            )
            from_after = passed_along(passing, "segment", -1)
    weight_grads = lax.psum(grad_sum.astype(jnp.bfloat16), "gy").astype(jnp.float32)
    return (feature_store[None], weight_grads[None], input_grads[None])


def solution(mesh):
    return jax.shard_map(
        local,
        mesh=mesh,
        in_specs=(
            P(None, None, None, "gy", None),
            P(None, None, None, "gy", None),
            P("segment", None, None, None, None),
        ),
        out_specs=(
            P("segment", None, None, None, "gy", None),
            P("segment", None, None, None, None),
            P("segment", None, None, None, "gy", None),
        ),
        check_vma=False,
    )
```

profile of v0, /device:TPU:0, one launch (start us, length us, event | category | flops | bytes accessed | tf_op | source)
XLA Modules:
  0.0 362.3 jit_solution(7427069599511536206)
XLA Ops:
  8.7 3.0 collective-permute-start.3
  15.1 3.0 collective-permute-done.1
  31.1 5.4 %collective-permute-done.4 = bf16[32,4,4,128]{3,0,2,1:T(8,128)(2,1)S(1)} collective-permute-done((bf16[32,4,4,128]{3,0,2,1:T(8,128)(2,1)S(1)}, bf16[32,4,4,128]{3,0,2,1:T(8,128)(2,1)S(1)}, u32[]{:S(2)}, u32[]{:S(2)}) %collective-permute-start.4) | collective-permute-done | bytes 131104 | tf_op jit(solution)/shard_map/ppermute | solution.py:21
  36.7 2.7 collective-permute-start.5
  42.1 2.6 collective-permute-done.6
  52.8 2.7 collective-permute-start.7
  58.1 6.1 %collective-permute-done.9 = bf16[32,4,4,128]{3,0,2,1:T(8,128)(2,1)S(1)} collective-permute-done((bf16[32,4,4,128]{3,0,2,1:T(8,128)(2,1)S(1)}, bf16[32,4,4,128]{3,0,2,1:T(8,128)(2,1)S(1)}, u32[]{:S(2)}, u32[]{:S(2)}) %collective-permute-start.9) | collective-permute-done | bytes 131104 | tf_op jit(solution)/shard_map/ppermute | solution.py:21
  64.3 2.6 collective-permute-start.10
  69.4 3.0 collective-permute-done.11
  80.5 2.9 collective-permute-start.12
  86.1 5.7 %collective-permute-done.14 = bf16[32,4,4,128]{3,0,2,1:T(8,128)(2,1)S(1)} collective-permute-done((bf16[32,4,4,128]{3,0,2,1:T(8,128)(2,1)S(1)}, bf16[32,4,4,128]{3,0,2,1:T(8,128)(2,1)S(1)}, u32[]{:S(2)}, u32[]{:S(2)}) %collective-permute-start.14) | collective-permute-done | bytes 131104 | tf_op jit(solution)/shard_map/ppermute | solution.py:21
  92.0 2.7 collective-permute-start.15
  115.1 4.1 %collective-permute-start.20 = (bf16[32,4,2,128]{3,0,2,1:T(8,128)(2,1)S(1)}, bf16[32,4,2,128]{3,0,2,1:T(8,128)(2,1)S(1)}, u32[]{:S(2)}, u32[]{:S(2)}) collective-permute-start(bf16[32,4,2,128]{3,0,2,1:T(8,128)(2,1)S(1)} %get-tuple-element.615), channel_id=1, source_target_pairs={{0,1},{1,2},{2,3},{3,4},{4,5},{5,6},{6,7},{8,9},{9,10},{10,11},{11... | collective-permute-start | bytes 196616 | tf_op jit(solution)/shard_map/ppermute | solution.py:12
  120.6 2.8 collective-permute-done.21
  131.4 4.8 %collective-permute-start.22 = (bf16[32,4,1,128]{3,0,2,1:T(8,128)(2,1)S(1)}, bf16[32,4,1,128]{3,0,2,1:T(8,128)(2,1)S(1)}, u32[]{:S(2)}, u32[]{:S(2)}) collective-permute-start(bf16[32,4,1,128]{3,0,2,1:T(8,128)(2,1)S(1)} %get-tuple-element.613), channel_id=1, source_target_pairs={{0,1},{1,2},{2,3},{3,4},{4,5},{5,6},{6,7},{8,9},{9,10},{10,11},{11... | collective-permute-start | bytes 98312 | tf_op jit(solution)/shard_map/ppermute | solution.py:12
  164.0 3.0 collective-permute-start.24
  175.5 3.1 collective-permute-start.31
  178.6 2.8 collective-permute-done.26
  181.6 4.5 %collective-permute-start.27 = (bf16[32,4,1,128]{3,0,2,1:T(8,128)(2,1)S(1)}, bf16[32,4,1,128]{3,0,2,1:T(8,128)(2,1)S(1)}, u32[]{:S(2)}, u32[]{:S(2)}) collective-permute-start(bf16[32,4,1,128]{3,0,2,1:T(8,128)(2,1)S(1)} %get-tuple-element.609), channel_id=1, source_target_pairs={{0,1},{1,2},{2,3},{3,4},{4,5},{5,6},{6,7},{8,9},{9,10},{10,11},{11... | collective-permute-start | bytes 98312 | tf_op jit(solution)/shard_map/ppermute | solution.py:12
  189.2 3.4 collective-permute-start.32
  195.8 3.6 %collective-permute-start.29 = (bf16[32,4,1,128]{3,0,2,1:T(8,128)(2,1)S(1)}, bf16[32,4,1,128]{3,0,2,1:T(8,128)(2,1)S(1)}, u32[]{:S(2)}, u32[]{:S(2)}) collective-permute-start(bf16[32,4,1,128]{3,0,2,1:T(8,128)(2,1)S(1)} %get-tuple-element.607), channel_id=1, source_target_pairs={{0,1},{1,2},{2,3},{3,4},{4,5},{5,6},{6,7},{8,9},{9,10},{10,11},{11... | collective-permute-start | bytes 98312 | tf_op jit(solution)/shard_map/ppermute | solution.py:12
  208.9 6.9 %collective-permute-done.33 = bf16[32,4,4,128]{3,0,2,1:T(8,128)(2,1)S(1)} collective-permute-done((bf16[32,4,4,128]{3,0,2,1:T(8,128)(2,1)S(1)}, bf16[32,4,4,128]{3,0,2,1:T(8,128)(2,1)S(1)}, u32[]{:S(2)}, u32[]{:S(2)}) %collective-permute-start.33) | collective-permute-done | bytes 131104 | tf_op jit(solution)/shard_map/ppermute | solution.py:27
  216.0 2.8 collective-permute-start.34
  226.1 4.8 %collective-permute-start.36 = (bf16[32,4,1,128]{3,0,2,1:T(8,128)(2,1)S(1)}, bf16[32,4,1,128]{3,0,2,1:T(8,128)(2,1)S(1)}, u32[]{:S(2)}, u32[]{:S(2)}) collective-permute-start(bf16[32,4,1,128]{3,0,2,1:T(8,128)(2,1)S(1)} %get-tuple-element.603), channel_id=1, source_target_pairs={{0,1},{1,2},{2,3},{3,4},{4,5},{5,6},{6,7},{8,9},{9,10},{10,11},{11... | collective-permute-start | bytes 98312 | tf_op jit(solution)/shard_map/ppermute | solution.py:12
  240.6 6.0 %collective-permute-done.40 = bf16[32,4,4,128]{3,0,2,1:T(8,128)(2,1)S(1)} collective-permute-done((bf16[32,4,4,128]{3,0,2,1:T(8,128)(2,1)S(1)}, bf16[32,4,4,128]{3,0,2,1:T(8,128)(2,1)S(1)}, u32[]{:S(2)}, u32[]{:S(2)}) %collective-permute-start.40) | collective-permute-done | bytes 131104 | tf_op jit(solution)/shard_map/ppermute | solution.py:27
  246.8 2.6 collective-permute-start.41
  256.5 4.5 %collective-permute-start.43 = (bf16[32,4,1,128]{3,0,2,1:T(8,128)(2,1)S(1)}, bf16[32,4,1,128]{3,0,2,1:T(8,128)(2,1)S(1)}, u32[]{:S(2)}, u32[]{:S(2)}) collective-permute-start(bf16[32,4,1,128]{3,0,2,1:T(8,128)(2,1)S(1)} %get-tuple-element.599), channel_id=1, source_target_pairs={{0,1},{1,2},{2,3},{3,4},{4,5},{5,6},{6,7},{8,9},{9,10},{10,11},{11... | collective-permute-start | bytes 98312 | tf_op jit(solution)/shard_map/ppermute | solution.py:12
  269.5 2.7 collective-permute-start.52
  272.3 2.7 collective-permute-done.47
  275.2 4.6 %collective-permute-start.48 = (bf16[32,4,1,128]{3,0,2,1:T(8,128)(2,1)S(1)}, bf16[32,4,1,128]{3,0,2,1:T(8,128)(2,1)S(1)}, u32[]{:S(2)}, u32[]{:S(2)}) collective-permute-start(bf16[32,4,1,128]{3,0,2,1:T(8,128)(2,1)S(1)} %get-tuple-element.597), channel_id=1, source_target_pairs={{0,1},{1,2},{2,3},{3,4},{4,5},{5,6},{6,7},{8,9},{9,10},{10,11},{11... | collective-permute-start | bytes 98312 | tf_op jit(solution)/shard_map/ppermute | solution.py:12
  287.0 4.8 %collective-permute-start.50 = (bf16[32,4,1,128]{3,0,2,1:T(8,128)(2,1)S(1)}, bf16[32,4,1,128]{3,0,2,1:T(8,128)(2,1)S(1)}, u32[]{:S(2)}, u32[]{:S(2)}) collective-permute-start(bf16[32,4,1,128]{3,0,2,1:T(8,128)(2,1)S(1)} %get-tuple-element.595), channel_id=1, source_target_pairs={{0,1},{1,2},{2,3},{3,4},{4,5},{5,6},{6,7},{8,9},{9,10},{10,11},{11... | collective-permute-start | bytes 98312 | tf_op jit(solution)/shard_map/ppermute | solution.py:12
  299.0 52.9 %all-reduce.22.cloned.1.call-done = bf16[1,2,27,32,32]{4,3,2,1,0:T(8,128)(2,1)} async-done(((bf16[1,2,27,32,32]{4,3,2,1,0:T(8,128)(2,1)}), bf16[1,2,27,32,32]{4,3,2,1,0:T(8,128)(2,1)}) %all-reduce.22.cloned.1.call-update) | async-done | bytes 110608 | tf_op jit(solution)/shard_map/psum | solution.py:204
  (793 shorter events, 172.7 us)
Async XLA Ops:
  7.2 344.7 %all-reduce.22.cloned.1.call-start = ((), (), s32[]{:S(2)}) async-start(), calls=%async_computation | async-start | bytes 884736 | tf_op jit(solution)/shard_map/psum | solution.py:204
  8.7 20.7 %collective-permute-start.3 = (bf16[32,4,4,128]{3,0,2,1:T(8,128)(2,1)S(1)}, bf16[32,4,4,128]{3,0,2,1:T(8,128)(2,1)S(1)}, u32[]{:S(2)}, u32[]{:S(2)}) collective-permute-start(bf16[32,4,4,128]{3,0,2,1:T(8,128)(2,1)S(1)} %fusion.577), channel_id=1, source_target_pairs={{0,8},{8,0},{16,24},{24,16},{1,9},{9,1},{17,25},{25,17},{2,10},{10... | collective-permute-start | bytes 393224 | tf_op jit(solution)/shard_map/ppermute | solution.py:21
  26.1 10.4 %collective-permute-start.2 = (bf16[32,4,4,128]{3,0,2,1:T(8,128)(2,1)S(1)}, bf16[32,4,4,128]{3,0,2,1:T(8,128)(2,1)S(1)}, u32[]{:S(2)}, u32[]{:S(2)}) collective-permute-start(bf16[32,4,4,128]{3,0,2,1:T(8,128)(2,1)S(1)} %get-tuple-element.35), channel_id=1, source_target_pairs={{0,8},{8,16},{16,24},{1,9},{9,17},{17,25},{2,10},{10,18},{18,26},{... | collective-permute-start | bytes 393224 | tf_op jit(solution)/shard_map/ppermute | solution.py:27
  29.5 7.0 %collective-permute-start.4 = (bf16[32,4,4,128]{3,0,2,1:T(8,128)(2,1)S(1)}, bf16[32,4,4,128]{3,0,2,1:T(8,128)(2,1)S(1)}, u32[]{:S(2)}, u32[]{:S(2)}) collective-permute-start(bf16[32,4,4,128]{3,0,2,1:T(8,128)(2,1)S(1)} %collective-permute-done.3), channel_id=1, source_target_pairs={{0,16},{8,24},{16,0},{24,8},{1,17},{9,25},{17,1},{25,9},{2,18},{10... | collective-permute-start | bytes 393224 | tf_op jit(solution)/shard_map/ppermute | solution.py:21
  40.9 15.3 %collective-permute-start.8 = (bf16[32,4,4,128]{3,0,2,1:T(8,128)(2,1)S(1)}, bf16[32,4,4,128]{3,0,2,1:T(8,128)(2,1)S(1)}, u32[]{:S(2)}, u32[]{:S(2)}) collective-permute-start(bf16[32,4,4,128]{3,0,2,1:T(8,128)(2,1)S(1)} %get-tuple-element.33), channel_id=1, source_target_pairs={{0,8},{8,0},{16,24},{24,16},{1,9},{9,1},{17,25},{25,17},{2,10},{10... | collective-permute-start | bytes 393224 | tf_op jit(solution)/shard_map/ppermute | solution.py:21
  52.8 11.4 %collective-permute-start.7 = (bf16[32,4,4,128]{3,0,2,1:T(8,128)(2,1)S(1)}, bf16[32,4,4,128]{3,0,2,1:T(8,128)(2,1)S(1)}, u32[]{:S(2)}, u32[]{:S(2)}) collective-permute-start(bf16[32,4,4,128]{3,0,2,1:T(8,128)(2,1)S(1)} %get-tuple-element.29), channel_id=1, source_target_pairs={{0,8},{8,16},{16,24},{1,9},{9,17},{17,25},{2,10},{10,18},{18,26},{... | collective-permute-start | bytes 393224 | tf_op jit(solution)/shard_map/ppermute | solution.py:27
  56.2 7.9 %collective-permute-start.9 = (bf16[32,4,4,128]{3,0,2,1:T(8,128)(2,1)S(1)}, bf16[32,4,4,128]{3,0,2,1:T(8,128)(2,1)S(1)}, u32[]{:S(2)}, u32[]{:S(2)}) collective-permute-start(bf16[32,4,4,128]{3,0,2,1:T(8,128)(2,1)S(1)} %collective-permute-done.8), channel_id=1, source_target_pairs={{0,16},{8,24},{16,0},{24,8},{1,17},{9,25},{17,1},{25,9},{2,18},{10... | collective-permute-start | bytes 393224 | tf_op jit(solution)/shard_map/ppermute | solution.py:21
  68.2 15.8 %collective-permute-start.13 = (bf16[32,4,4,128]{3,0,2,1:T(8,128)(2,1)S(1)}, bf16[32,4,4,128]{3,0,2,1:T(8,128)(2,1)S(1)}, u32[]{:S(2)}, u32[]{:S(2)}) collective-permute-start(bf16[32,4,4,128]{3,0,2,1:T(8,128)(2,1)S(1)} %get-tuple-element.27), channel_id=1, source_target_pairs={{0,8},{8,0},{16,24},{24,16},{1,9},{9,1},{17,25},{25,17},{2,10},{10... | collective-permute-start | bytes 393224 | tf_op jit(solution)/shard_map/ppermute | solution.py:21
  80.5 11.4 %collective-permute-start.12 = (bf16[32,4,4,128]{3,0,2,1:T(8,128)(2,1)S(1)}, bf16[32,4,4,128]{3,0,2,1:T(8,128)(2,1)S(1)}, u32[]{:S(2)}, u32[]{:S(2)}) collective-permute-start(bf16[32,4,4,128]{3,0,2,1:T(8,128)(2,1)S(1)} %get-tuple-element.23), channel_id=1, source_target_pairs={{0,8},{8,16},{16,24},{1,9},{9,17},{17,25},{2,10},{10,18},{18,26},{... | collective-permute-start | bytes 393224 | tf_op jit(solution)/shard_map/ppermute | solution.py:27
  84.1 7.7 %collective-permute-start.14 = (bf16[32,4,4,128]{3,0,2,1:T(8,128)(2,1)S(1)}, bf16[32,4,4,128]{3,0,2,1:T(8,128)(2,1)S(1)}, u32[]{:S(2)}, u32[]{:S(2)}) collective-permute-start(bf16[32,4,4,128]{3,0,2,1:T(8,128)(2,1)S(1)} %collective-permute-done.13), channel_id=1, source_target_pairs={{0,16},{8,24},{16,0},{24,8},{1,17},{9,25},{17,1},{25,9},{2,18},{10... | collective-permute-start | bytes 393224 | tf_op jit(solution)/shard_map/ppermute | solution.py:21
  96.0 12.7 %collective-permute-start.18 = (bf16[32,4,4,128]{3,0,2,1:T(8,128)(2,1)S(1)}, bf16[32,4,4,128]{3,0,2,1:T(8,128)(2,1)S(1)}, u32[]{:S(2)}, u32[]{:S(2)}) collective-permute-start(bf16[32,4,4,128]{3,0,2,1:T(8,128)(2,1)S(1)} %get-tuple-element.21), channel_id=1, source_target_pairs={{0,8},{8,0},{16,24},{24,16},{1,9},{9,1},{17,25},{25,17},{2,10},{10... | collective-permute-start | bytes 393224 | tf_op jit(solution)/shard_map/ppermute | solution.py:21
  131.4 29.1 %collective-permute-start.22 = (bf16[32,4,1,128]{3,0,2,1:T(8,128)(2,1)S(1)}, bf16[32,4,1,128]{3,0,2,1:T(8,128)(2,1)S(1)}, u32[]{:S(2)}, u32[]{:S(2)}) collective-permute-start(bf16[32,4,1,128]{3,0,2,1:T(8,128)(2,1)S(1)} %get-tuple-element.613), channel_id=1, source_target_pairs={{0,1},{1,2},{2,3},{3,4},{4,5},{5,6},{6,7},{8,9},{9,10},{10,11},{11... | collective-permute-start | bytes 98312 | tf_op jit(solution)/shard_map/ppermute | solution.py:12
  136.3 24.3 %collective-permute-start.23 = (bf16[32,4,1,128]{3,0,2,1:T(8,128)(2,1)S(1)}, bf16[32,4,1,128]{3,0,2,1:T(8,128)(2,1)S(1)}, u32[]{:S(2)}, u32[]{:S(2)}) collective-permute-start(bf16[32,4,1,128]{3,0,2,1:T(8,128)(2,1)S(1)} %get-tuple-element.614), channel_id=1, source_target_pairs={{1,0},{2,1},{3,2},{4,3},{5,4},{6,5},{7,6},{9,8},{10,9},{11,10},{12... | collective-permute-start | bytes 98312 | tf_op jit(solution)/shard_map/ppermute | solution.py:15
  174.1 7.3 %collective-permute-start.26 = (bf16[32,4,4,128]{3,0,2,1:T(8,128)(2,1)S(1)}, bf16[32,4,4,128]{3,0,2,1:T(8,128)(2,1)S(1)}, u32[]{:S(2)}, u32[]{:S(2)}) collective-permute-start(bf16[32,4,4,128]{3,0,2,1:T(8,128)(2,1)S(1)} %get-tuple-element.13), channel_id=1, source_target_pairs={{8,0},{16,8},{24,16},{9,1},{17,9},{25,17},{10,2},{18,10},{26,18},{... | collective-permute-start | bytes 393224 | tf_op jit(solution)/shard_map/ppermute | solution.py:27
  175.5 13.7 %collective-permute-start.31 = (bf16[32,4,4,128]{3,0,2,1:T(8,128)(2,1)S(1)}, bf16[32,4,4,128]{3,0,2,1:T(8,128)(2,1)S(1)}, u32[]{:S(2)}, u32[]{:S(2)}) collective-permute-start(bf16[32,4,4,128]{3,0,2,1:T(8,128)(2,1)S(1)} %get-tuple-element.13), channel_id=1, source_target_pairs={{0,8},{8,0},{16,24},{24,16},{1,9},{9,1},{17,25},{25,17},{2,10},{10... | collective-permute-start | bytes 393224 | tf_op jit(solution)/shard_map/ppermute | solution.py:21
  181.6 11.0 %collective-permute-start.27 = (bf16[32,4,1,128]{3,0,2,1:T(8,128)(2,1)S(1)}, bf16[32,4,1,128]{3,0,2,1:T(8,128)(2,1)S(1)}, u32[]{:S(2)}, u32[]{:S(2)}) collective-permute-start(bf16[32,4,1,128]{3,0,2,1:T(8,128)(2,1)S(1)} %get-tuple-element.609), channel_id=1, source_target_pairs={{0,1},{1,2},{2,3},{3,4},{4,5},{5,6},{6,7},{8,9},{9,10},{10,11},{11... | collective-permute-start | bytes 98312 | tf_op jit(solution)/shard_map/ppermute | solution.py:12
  186.1 6.5 %collective-permute-start.28 = (bf16[32,4,1,128]{3,0,2,1:T(8,128)(2,1)S(1)}, bf16[32,4,1,128]{3,0,2,1:T(8,128)(2,1)S(1)}, u32[]{:S(2)}, u32[]{:S(2)}) collective-permute-start(bf16[32,4,1,128]{3,0,2,1:T(8,128)(2,1)S(1)} %get-tuple-element.610), channel_id=1, source_target_pairs={{1,0},{2,1},{3,2},{4,3},{5,4},{6,5},{7,6},{9,8},{10,9},{11,10},{12... | collective-permute-start | bytes 98312 | tf_op jit(solution)/shard_map/ppermute | solution.py:15
  189.2 18.0 %collective-permute-start.32 = (bf16[32,4,4,128]{3,0,2,1:T(8,128)(2,1)S(1)}, bf16[32,4,4,128]{3,0,2,1:T(8,128)(2,1)S(1)}, u32[]{:S(2)}, u32[]{:S(2)}) collective-permute-start(bf16[32,4,4,128]{3,0,2,1:T(8,128)(2,1)S(1)} %collective-permute-done.31), channel_id=1, source_target_pairs={{0,16},{8,24},{16,0},{24,8},{1,17},{9,25},{17,1},{25,9},{2,18},{10... | collective-permute-start | bytes 393224 | tf_op jit(solution)/shard_map/ppermute | solution.py:21
  207.4 14.1 %collective-permute-start.38 = (bf16[32,4,4,128]{3,0,2,1:T(8,128)(2,1)S(1)}, bf16[32,4,4,128]{3,0,2,1:T(8,128)(2,1)S(1)}, u32[]{:S(2)}, u32[]{:S(2)}) collective-permute-start(bf16[32,4,4,128]{3,0,2,1:T(8,128)(2,1)S(1)} %get-tuple-element.11), channel_id=1, source_target_pairs={{0,8},{8,0},{16,24},{24,16},{1,9},{9,1},{17,25},{25,17},{2,10},{10... | collective-permute-start | bytes 393224 | tf_op jit(solution)/shard_map/ppermute | solution.py:21
  207.5 8.3 %collective-permute-start.33 = (bf16[32,4,4,128]{3,0,2,1:T(8,128)(2,1)S(1)}, bf16[32,4,4,128]{3,0,2,1:T(8,128)(2,1)S(1)}, u32[]{:S(2)}, u32[]{:S(2)}) collective-permute-start(bf16[32,4,4,128]{3,0,2,1:T(8,128)(2,1)S(1)} %fusion.277), channel_id=1, source_target_pairs={{8,0},{16,8},{24,16},{9,1},{17,9},{25,17},{10,2},{18,10},{26,18},{... | collective-permute-start | bytes 393224 | tf_op jit(solution)/shard_map/ppermute | solution.py:27
  221.5 15.6 %collective-permute-start.39 = (bf16[32,4,4,128]{3,0,2,1:T(8,128)(2,1)S(1)}, bf16[32,4,4,128]{3,0,2,1:T(8,128)(2,1)S(1)}, u32[]{:S(2)}, u32[]{:S(2)}) collective-permute-start(bf16[32,4,4,128]{3,0,2,1:T(8,128)(2,1)S(1)} %collective-permute-done.38), channel_id=1, source_target_pairs={{0,16},{8,24},{16,0},{24,8},{1,17},{9,25},{17,1},{25,9},{2,18},{10... | collective-permute-start | bytes 393224 | tf_op jit(solution)/shard_map/ppermute | solution.py:21
  226.1 7.7 %collective-permute-start.36 = (bf16[32,4,1,128]{3,0,2,1:T(8,128)(2,1)S(1)}, bf16[32,4,1,128]{3,0,2,1:T(8,128)(2,1)S(1)}, u32[]{:S(2)}, u32[]{:S(2)}) collective-permute-start(bf16[32,4,1,128]{3,0,2,1:T(8,128)(2,1)S(1)} %get-tuple-element.603), channel_id=1, source_target_pairs={{0,1},{1,2},{2,3},{3,4},{4,5},{5,6},{6,7},{8,9},{9,10},{10,11},{11... | collective-permute-start | bytes 98312 | tf_op jit(solution)/shard_map/ppermute | solution.py:12
  237.4 14.7 %collective-permute-start.45 = (bf16[32,4,4,128]{3,0,2,1:T(8,128)(2,1)S(1)}, bf16[32,4,4,128]{3,0,2,1:T(8,128)(2,1)S(1)}, u32[]{:S(2)}, u32[]{:S(2)}) collective-permute-start(bf16[32,4,4,128]{3,0,2,1:T(8,128)(2,1)S(1)} %get-tuple-element.9), channel_id=1, source_target_pairs={{0,8},{8,0},{16,24},{24,16},{1,9},{9,1},{17,25},{25,17},{2,10},{10... | collective-permute-start | bytes 393224 | tf_op jit(solution)/shard_map/ppermute | solution.py:21
  239.3 7.3 %collective-permute-start.40 = (bf16[32,4,4,128]{3,0,2,1:T(8,128)(2,1)S(1)}, bf16[32,4,4,128]{3,0,2,1:T(8,128)(2,1)S(1)}, u32[]{:S(2)}, u32[]{:S(2)}) collective-permute-start(bf16[32,4,4,128]{3,0,2,1:T(8,128)(2,1)S(1)} %fusion.276), channel_id=1, source_target_pairs={{8,0},{16,8},{24,16},{9,1},{17,9},{25,17},{10,2},{18,10},{26,18},{... | collective-permute-start | bytes 393224 | tf_op jit(solution)/shard_map/ppermute | solution.py:27
  246.8 6.5 %collective-permute-start.41 = (bf16[32,4,1,128]{3,0,2,1:T(8,128)(2,1)S(1)}, bf16[32,4,1,128]{3,0,2,1:T(8,128)(2,1)S(1)}, u32[]{:S(2)}, u32[]{:S(2)}) collective-permute-start(bf16[32,4,1,128]{3,0,2,1:T(8,128)(2,1)S(1)} %get-tuple-element.601), channel_id=1, source_target_pairs={{0,1},{1,2},{2,3},{3,4},{4,5},{5,6},{6,7},{8,9},{9,10},{10,11},{11... | collective-permute-start | bytes 98312 | tf_op jit(solution)/shard_map/ppermute | solution.py:12
  252.1 15.8 %collective-permute-start.46 = (bf16[32,4,4,128]{3,0,2,1:T(8,128)(2,1)S(1)}, bf16[32,4,4,128]{3,0,2,1:T(8,128)(2,1)S(1)}, u32[]{:S(2)}, u32[]{:S(2)}) collective-permute-start(bf16[32,4,4,128]{3,0,2,1:T(8,128)(2,1)S(1)} %collective-permute-done.45), channel_id=1, source_target_pairs={{0,16},{8,24},{16,0},{24,8},{1,17},{9,25},{17,1},{25,9},{2,18},{10... | collective-permute-start | bytes 393224 | tf_op jit(solution)/shard_map/ppermute | solution.py:21
  256.5 7.2 %collective-permute-start.43 = (bf16[32,4,1,128]{3,0,2,1:T(8,128)(2,1)S(1)}, bf16[32,4,1,128]{3,0,2,1:T(8,128)(2,1)S(1)}, u32[]{:S(2)}, u32[]{:S(2)}) collective-permute-start(bf16[32,4,1,128]{3,0,2,1:T(8,128)(2,1)S(1)} %get-tuple-element.599), channel_id=1, source_target_pairs={{0,1},{1,2},{2,3},{3,4},{4,5},{5,6},{6,7},{8,9},{9,10},{10,11},{11... | collective-permute-start | bytes 98312 | tf_op jit(solution)/shard_map/ppermute | solution.py:12
  268.2 6.9 %collective-permute-start.47 = (bf16[32,4,4,128]{3,0,2,1:T(8,128)(2,1)S(1)}, bf16[32,4,4,128]{3,0,2,1:T(8,128)(2,1)S(1)}, u32[]{:S(2)}, u32[]{:S(2)}) collective-permute-start(bf16[32,4,4,128]{3,0,2,1:T(8,128)(2,1)S(1)} %fusion.275), channel_id=1, source_target_pairs={{8,0},{16,8},{24,16},{9,1},{17,9},{25,17},{10,2},{18,10},{26,18},{... | collective-permute-start | bytes 393224 | tf_op jit(solution)/shard_map/ppermute | solution.py:27
  269.5 13.1 %collective-permute-start.52 = (bf16[32,4,4,128]{3,0,2,1:T(8,128)(2,1)S(1)}, bf16[32,4,4,128]{3,0,2,1:T(8,128)(2,1)S(1)}, u32[]{:S(2)}, u32[]{:S(2)}) collective-permute-start(bf16[32,4,4,128]{3,0,2,1:T(8,128)(2,1)S(1)} %get-tuple-element.7), channel_id=1, source_target_pairs={{0,8},{8,0},{16,24},{24,16},{1,9},{9,1},{17,25},{25,17},{2,10},{10... | collective-permute-start | bytes 393224 | tf_op jit(solution)/shard_map/ppermute | solution.py:21
  275.2 8.1 %collective-permute-start.48 = (bf16[32,4,1,128]{3,0,2,1:T(8,128)(2,1)S(1)}, bf16[32,4,1,128]{3,0,2,1:T(8,128)(2,1)S(1)}, u32[]{:S(2)}, u32[]{:S(2)}) collective-permute-start(bf16[32,4,1,128]{3,0,2,1:T(8,128)(2,1)S(1)} %get-tuple-element.597), channel_id=1, source_target_pairs={{0,1},{1,2},{2,3},{3,4},{4,5},{5,6},{6,7},{8,9},{9,10},{10,11},{11... | collective-permute-start | bytes 98312 | tf_op jit(solution)/shard_map/ppermute | solution.py:12
  282.7 71.2 %collective-permute-start.53 = (bf16[32,4,4,128]{3,0,2,1:T(8,128)(2,1)S(1)}, bf16[32,4,4,128]{3,0,2,1:T(8,128)(2,1)S(1)}, u32[]{:S(2)}, u32[]{:S(2)}) collective-permute-start(bf16[32,4,4,128]{3,0,2,1:T(8,128)(2,1)S(1)} %collective-permute-done.52), channel_id=1, source_target_pairs={{0,16},{8,24},{16,0},{24,8},{1,17},{9,25},{17,1},{25,9},{2,18},{10... | collective-permute-start | bytes 393224 | tf_op jit(solution)/shard_map/ppermute | solution.py:21
  287.0 8.9 %collective-permute-start.50 = (bf16[32,4,1,128]{3,0,2,1:T(8,128)(2,1)S(1)}, bf16[32,4,1,128]{3,0,2,1:T(8,128)(2,1)S(1)}, u32[]{:S(2)}, u32[]{:S(2)}) collective-permute-start(bf16[32,4,1,128]{3,0,2,1:T(8,128)(2,1)S(1)} %get-tuple-element.595), channel_id=1, source_target_pairs={{0,1},{1,2},{2,3},{3,4},{4,5},{5,6},{6,7},{8,9},{9,10},{10,11},{11... | collective-permute-start | bytes 98312 | tf_op jit(solution)/shard_map/ppermute | solution.py:12
  (25 other events, 122.2 us)
Sparse Core Ops, SparseCore 0:
  296.0 55.8 all-reduce.21
where the time goes:
time: 369 us; the launch traced here: 362 us
  starting transfers between devices  117 us (32%)
  waiting for transfers between devices  111 us (30%)
  local copies, waits for them, and re-layouts  63.7 us (17%)
  matrix products  36.7 us (10%)
  between operations  19.6 us (5%)
  other arithmetic  14.5 us (4%)
    ppermute x15, starting transfers between devices, extended(): lax.ppermute(lax.slice_in_dim(block, block.shape[dim] - width, None, axis...  53.8 us
    psum x1, waiting for transfers between devices, local(): lax.psum(grad_sum.astype(jnp.bfloat16), 'gy').astype(jnp.float32)  52.9 us
    unnamed x379, local copies, waits for them, and re-layouts  47.9 us
    ppermute x16, starting transfers between devices, from_partner(): lax.ppermute(array, axis, [(i, i ^ 1 << bit) for i in range(lax.axis_size...  28.4 us
    dot_general x60, matrix products, convolve(): jnp.einsum('tczyx,tco->ozyx', slices_of(padded, plane_shift, row_count),...  23.6 us
    ppermute x15, starting transfers between devices, extended(): lax.ppermute(lax.slice_in_dim(block, 0, width, axis=dim), axis, backward)  20.5 us
    ppermute x15, waiting for transfers between devices, extended(): lax.ppermute(lax.slice_in_dim(block, 0, width, axis=dim), axis, backward)  19.7 us
    ppermute x8, waiting for transfers between devices, passed_along(): lax.ppermute(value, axis, [(source, source + steps) for source in range(f...  19.3 us
  transfers between devices with their start and end apart: 55, of which 21 were waited for; matrix products, arithmetic and copies ran while one was open for 27% of the time, Pallas kernels for 0%

commit v1 on v0

v1 whole, which is shorter than its diff:
```python
import functools

import jax
import jax.numpy as jnp
from jax import lax
from jax.experimental import pallas as pl
from jax.experimental.pallas import tpu as pltpu
from jax.sharding import PartitionSpec as P

HALO = 2


def shifted_fields(value):
    across = value.shape[1]
    lane = lax.broadcasted_iota(jnp.int32, value.shape, 1)
    left = jnp.where(lane == 0, 0.0, pltpu.roll(value, 1, 1))
    right = jnp.where(lane == across - 1, 0.0, pltpu.roll(value, across - 1, 1))
    return [v.astype(jnp.bfloat16) for v in (left, value, right)]


def fill_columns(col, planes_of, planes):
    across = col.shape[-1] // 2
    frame = col.shape[2]
    zero = jnp.zeros((frame, across), jnp.bfloat16)
    for dx in range(3):
        col[dx, 0, :, :across] = zero
        col[dx, planes, :, across:] = zero
    for z in range(planes):
        for dx, field in enumerate(shifted_fields(planes_of(z))):
            col[dx, z + 1, :, :across] = field
            col[dx, z, :, across:] = field


def build_taps(taps, compact, out_rows):
    channels = compact.shape[1]
    frame = taps.shape[2]
    for j in range(9):
        wide = jnp.concatenate(
            [
                compact[j].astype(jnp.float32),
                jnp.zeros((channels, frame - compact.shape[2]), jnp.float32),
            ],
            1,
        )
        for y in range(out_rows):
            moved = wide if y == 0 else pltpu.roll(wide, y * channels, 1)
            taps[j, y * channels : (y + 1) * channels, :] = moved.astype(jnp.bfloat16)


def convolved(taps, col, pair, low, high):
    total = None
    for dz in range(3):
        for dx in range(3):
            part = jnp.dot(
                taps[3 * dz + dx, low:high, :],
                col[dx, 2 * pair + dz],
                preferred_element_type=jnp.float32,
            )
            total = part if total is None else total + part
    return total


def logistic_of(value):
    return 1.0 / (1.0 + jnp.exp(-value))


def row_mask(channels, rows, frame_start, inside_low, inside_high, across):
    row = lax.broadcasted_iota(jnp.int32, (rows * channels, across), 0) // channels + frame_start
    return (row >= inside_low) & (row < inside_high)


def forward_kernel(
    sizes, with_skip, low_ref, mid_ref, high_ref, first_ref, second_ref, *rest
):
    channels, planes, rows, across = sizes
    if with_skip:
        skip_ref, *rest = rest
    (features_ref, next_ref, frame_ref, hidden_ref, slope1_ref, slope2_ref, col, taps) = rest
    gy = lax.axis_index("gy")
    count = lax.axis_size("gy")
    inner = rows + 2
    inside_low = jnp.where(gy == 0, HALO, 0)
    inside_high = jnp.where(gy == count - 1, rows + HALO, rows + 2 * HALO)
    for z in range(planes):
        frame_ref[z, : HALO * channels] = low_ref[z]
        frame_ref[z, HALO * channels : (HALO + rows) * channels] = mid_ref[z]
        frame_ref[z, (HALO + rows) * channels :] = high_ref[z]
    fill_columns(col, lambda z: frame_ref[z].astype(jnp.float32), planes)
    build_taps(taps, first_ref, inner)
    mask = row_mask(channels, inner, 1, inside_low, inside_high, across)
    edge = jnp.zeros((channels, across), jnp.bfloat16)
    for pair in range(planes // 2):
        pre = convolved(taps, col, pair, 0, inner * channels)
        for half in range(2):
            z = 2 * pair + half
            part = pre[:, half * across : (half + 1) * across]
            logistic = logistic_of(part)
            slope1_ref[z] = logistic * (1.0 + part * (1.0 - logistic))
            hidden_ref[z, :channels] = edge
            hidden_ref[z, channels : (inner + 1) * channels] = jnp.where(
                mask, part * logistic, 0.0
            ).astype(jnp.bfloat16)
            hidden_ref[z, (inner + 1) * channels :] = edge
    fill_columns(col, lambda z: hidden_ref[z].astype(jnp.float32), planes)
    build_taps(taps, second_ref, inner)
    for pair in range(planes // 2):
        pre = convolved(taps, col, pair, channels, (rows + 1) * channels)
        for half in range(2):
            z = 2 * pair + half
            part = pre[:, half * across : (half + 1) * across]
            logistic = logistic_of(part)
            slope2_ref[z] = logistic * (1.0 + part * (1.0 - logistic))
            leaving = (part * logistic).astype(jnp.bfloat16)
            features_ref[z] = leaving
            if with_skip:
                leaving = (
                    leaving.astype(jnp.float32) + skip_ref[z].astype(jnp.float32)
                ).astype(jnp.bfloat16)
            next_ref[z] = leaving


def backward_kernel(
    sizes, with_extra, with_next, low_ref, mid_ref, high_ref, first_ref, second_ref, slope1_ref, *rest
):
    channels, planes, rows, across = sizes
    if with_extra:
        extra_ref, *rest = rest
    if with_next:
        slope2_ref, *rest = rest
        (grads_ref, first_delta_ref, next_ref, wide, col, taps) = rest
    else:
        (grads_ref, first_delta_ref, wide, col, taps) = rest
    gy = lax.axis_index("gy")
    count = lax.axis_size("gy")
    inner = rows + 2
    inside_low = jnp.where(gy == 0, HALO, 0)
    inside_high = jnp.where(gy == count - 1, rows + HALO, rows + 2 * HALO)
    for z in range(planes):
        wide[z, : HALO * channels] = low_ref[z]
        wide[z, HALO * channels : (HALO + rows) * channels] = mid_ref[z]
        wide[z, (HALO + rows) * channels :] = high_ref[z]
    fill_columns(col, lambda z: wide[z].astype(jnp.float32), planes)
    build_taps(taps, second_ref, inner)
    mask = row_mask(channels, inner, 1, inside_low, inside_high, across)
    edge = jnp.zeros((channels, across), jnp.bfloat16)
    for pair in range(planes // 2):
        pre = convolved(taps, col, pair, 0, inner * channels)
        for half in range(2):
            z = 2 * pair + half
            part = pre[:, half * across : (half + 1) * across]
            delta = jnp.where(mask, part * slope1_ref[z], 0.0).astype(jnp.bfloat16)
            wide[z, :channels] = edge
            wide[z, channels : (inner + 1) * channels] = delta
            wide[z, (inner + 1) * channels :] = edge
            first_delta_ref[z] = delta[channels : (rows + 1) * channels]
    fill_columns(col, lambda z: wide[z].astype(jnp.float32), planes)
    build_taps(taps, first_ref, inner)
    for pair in range(planes // 2):
        pre = convolved(taps, col, pair, channels, (rows + 1) * channels)
        for half in range(2):
            z = 2 * pair + half
            value = pre[:, half * across : (half + 1) * across].astype(jnp.bfloat16)
            if with_extra:
                value = (
                    value.astype(jnp.float32) + extra_ref[z].astype(jnp.float32)
                ).astype(jnp.bfloat16)
            grads_ref[z] = value
            if with_next:
                next_ref[z] = (value.astype(jnp.float32) * slope2_ref[z]).astype(jnp.bfloat16)


def weight_kernel(sizes, frame_ref, first_ref, hidden_ref, second_ref, out_ref, columns):
    channels, planes, rows, across = sizes
    zero = jnp.zeros((channels, rows * across), jnp.bfloat16)
    for index, (source, delta) in enumerate(((frame_ref, first_ref), (hidden_ref, second_ref))):
        for z in range(planes):
            fields = shifted_fields(source[z].astype(jnp.float32))
            for dx, field in enumerate(fields):
                for dy in range(3):
                    block = jnp.concatenate(
                        [
                            field[(y + 1 + dy) * channels : (y + 2 + dy) * channels]
                            for y in range(rows)
                        ],
                        1,
                    )
                    for dz in range(3):
                        target = z + 1 - dz
                        if 0 <= target < planes:
                            tap = (9 * dz + 3 * dy + dx) * channels
                            columns[
                                tap : tap + channels,
                                target * rows * across : (target + 1) * rows * across,
                            ] = block
        for dz, target in ((0, 0), (2, planes - 1)):
            for tap in range(9 * dz, 9 * dz + 9):
                columns[
                    tap * channels : (tap + 1) * channels,
                    target * rows * across : (target + 1) * rows * across,
                ] = zero
        right = jnp.concatenate(
            [
                delta[z, y * channels : (y + 1) * channels, :]
                for z in range(planes)
                for y in range(rows)
            ],
            1,
        )
        out_ref[index] = lax.dot_general(
            right, columns[...], (((1,), (1,)), ((), ())), preferred_element_type=jnp.float32
        )


def with_halos(block, channels):
    count = lax.axis_size("gy")
    width = HALO * channels
    forward = [(i, i + 1) for i in range(count - 1)]
    backward = [(i + 1, i) for i in range(count - 1)]
    low = lax.ppermute(block[:, -width:], "gy", forward)
    high = lax.ppermute(block[:, :width], "gy", backward)
    return low, block, high


def partner(array, axis, mask):
    return lax.ppermute(array, axis, [(i, i ^ mask) for i in range(lax.axis_size(axis))])


def local(crops, cotangent, weights):
    micro_count, channels, planes, rows, across = crops.shape
    sizes = (channels, planes, rows, across)
    segment = lax.axis_index("segment")
    sections = lax.axis_size("segment")
    micro = segment % 2
    upper = segment >= 2
    inner = rows + 2
    frame = (rows + 2 * HALO) * channels
    spec = pl.BlockSpec(memory_space=pltpu.VMEM)
    bf = lambda *shape: jax.ShapeDtypeStruct(shape, jnp.bfloat16)
    fl = lambda *shape: jax.ShapeDtypeStruct(shape, jnp.float32)
    params = pltpu.CompilerParams(vmem_limit_bytes=48 * 2**20)
    column_scratch = pltpu.VMEM((3, planes + 1, frame, 2 * across), jnp.bfloat16)
    tap_scratch = pltpu.VMEM((9, inner * channels, frame), jnp.bfloat16)

    kernels = weights[0].reshape(2, 3, 3, 3, channels, channels)
    straight = jnp.transpose(kernels, (0, 1, 3, 5, 2, 4))
    turned = jnp.transpose(jnp.flip(kernels, (1, 2, 3)), (0, 1, 3, 4, 2, 5))
    compact = jnp.stack([straight, turned], 1).reshape(2, 2, 9, channels, 3 * channels)
    compact = jnp.pad(compact, ((0, 0),) * 4 + ((0, 128 - 3 * channels),))
    gathered = [compact]
    for step in range(1, sections):
        gathered.append(
            lax.ppermute(
                compact, "segment", [(i, (i + step) % sections) for i in range(sections)]
            )
        )
    gathered = jnp.stack(gathered)
    by_section = [
        lax.dynamic_index_in_dim(gathered, (segment - s) % sections, 0, keepdims=False)
        for s in range(sections)
    ]

    def arranged(field):
        mine = lax.dynamic_index_in_dim(field, micro, 0, keepdims=False)
        return jnp.transpose(mine, (1, 2, 0, 3)).reshape(planes, rows * channels, across)

    def restored(field):
        return jnp.transpose(
            field.reshape(planes, rows, channels, across), (2, 0, 1, 3)
        )

    merged = arranged(crops)
    outgoing = arranged(cotangent)
    band = (planes, rows * channels, across)
    entering = [merged]
    features, frames, hiddens, slopes1, slopes2 = [], [], [], [], []
    for s in range(sections):
        skip = entering[2 - s] if s in (1, 2) else None
        operands = list(with_halos(merged, channels)) + [by_section[s][0, 0], by_section[s][1, 0]]
        if skip is not None:
            operands.append(skip)
        leaving, merged, wide, hidden, slope1, slope2 = pl.pallas_call(
            functools.partial(forward_kernel, sizes, skip is not None),
            out_shape=(
                bf(*band),
                bf(*band),
                bf(planes, frame, across),
                bf(planes, frame, across),
                fl(planes, inner * channels, across),
                fl(*band),
            ),
            in_specs=[spec] * len(operands),
            out_specs=(spec,) * 6,
            scratch_shapes=[column_scratch, tap_scratch],
            compiler_params=params,
        )(*operands)
        entering.append(leaving)
        features.append(leaving)
        frames.append(wide)
        hiddens.append(hidden)
        slopes1.append(slope1)
        slopes2.append(slope2)

    second = (outgoing.astype(jnp.float32) * slopes2[-1]).astype(jnp.bfloat16)
    seconds = [None] * sections
    firsts = [None] * sections
    grads = [None] * sections
    for s in reversed(range(sections)):
        seconds[s] = second
        operands = list(with_halos(second, channels)) + [
            by_section[s][0, 1],
            by_section[s][1, 1],
            slopes1[s],
        ]
        outs = [bf(*band), bf(*band)]
        if s < 2:
            operands.append(grads[3 - s])
        if s > 0:
            operands.append(slopes2[s - 1])
            outs.append(bf(*band))
        result = pl.pallas_call(
            functools.partial(backward_kernel, sizes, s < 2, s > 0),
            out_shape=tuple(outs),
            in_specs=[spec] * len(operands),
            out_specs=(spec,) * len(outs),
            scratch_shapes=[
                pltpu.VMEM((planes, frame, across), jnp.bfloat16),
                column_scratch,
                tap_scratch,
            ],
            compiler_params=params,
        )(*operands)
        grads[s], firsts[s] = result[0], result[1]
        if s > 0:
            second = result[2]

    def own(values):
        pair = [jnp.where(upper, values[k + 2], values[k]) for k in range(2)]
        keep = jnp.where(micro == 0, pair[0], pair[1])
        give = jnp.where(micro == 0, pair[1], pair[0])
        return keep, give

    def weight_terms(values):
        picked = [jnp.where(upper, values[k + 2], values[k]) for k in range(2)]
        return picked

    picked = [weight_terms(v) for v in (frames, firsts, hiddens, seconds)]
    terms = []
    for k in range(2):
        terms.append(
            pl.pallas_call(
                functools.partial(weight_kernel, sizes),
                out_shape=fl(2, channels, 27 * channels),
                in_specs=[spec] * 4,
                out_specs=spec,
                scratch_shapes=[
                    pltpu.VMEM((27 * channels, planes * rows * across), jnp.bfloat16)
                ],
                compiler_params=params,
            )(*[p[k] for p in picked])
        )
    keep = jnp.where(micro == 0, terms[0], terms[1])
    give = jnp.where(micro == 0, terms[1], terms[0])
    total = keep + partner(give.astype(jnp.bfloat16), "segment", 1).astype(jnp.float32)
    count = lax.axis_size("gy")
    mask = 1
    while mask < count:
        total = total + partner(total.astype(jnp.bfloat16), "gy", mask).astype(jnp.float32)
        mask *= 2
    weight_grads = jnp.transpose(
        total.reshape(2, channels, 27, channels), (0, 2, 3, 1)
    )

    def both(values):
        keep, give = own(values)
        come = partner(give, "segment", 1)
        first = jnp.where(micro == 0, keep, come)
        last = jnp.where(micro == 0, come, keep)
        return jnp.stack([restored(first), restored(last)])

    return (
        both(features)[None],
        weight_grads[None],
        both(grads).astype(jnp.float32)[None],
    )


def solution(mesh):
    return jax.shard_map(
        local,
        mesh=mesh,
        in_specs=(
            P(None, None, None, "gy", None),
            P(None, None, None, "gy", None),
            P("segment", None, None, None, None),
        ),
        out_specs=(
            P("segment", None, None, None, "gy", None),
            P("segment", None, None, None, None),
            P("segment", None, None, None, "gy", None),
        ),
        check_vma=False,
    )
```

time: 369 us -> 114 us (0.31); the launches traced: 362 us -> 114 us
  waiting for transfers between devices: 111 us -> 20.6 us
  local copies, waits for them, and re-layouts: 63.7 us -> 6.71 us
  starting transfers between devices: 117 us -> 64.8 us
  matrix products: 36.7 us -> 0 us
  between operations: 19.6 us -> 1.38 us
  Pallas kernels: 0 us -> 17.6 us
  other arithmetic: 14.5 us -> 2.67 us
    psum x1 -> x0, waiting for transfers between devices: 52.9 us -> none  [local(): lax.psum(grad_sum.astype(jnp.bfloat16), 'gy').astype(jnp.float32)]
    ppermute x54 -> x25, starting transfers between devices: 117 us -> 64.8 us  [the longest x8 36 us: with_halos(): low = lax.ppermute(block[:, -width:], 'gy', forward)]
    unnamed x379 -> x8, local copies, waits for them, and re-layouts: 47.9 us -> 1.47 us
    ppermute x54 -> x25, waiting for transfers between devices: 57.7 us -> 20.6 us  [the longest x6 9.87 us: partner(): lax.ppermute(array, axis, [(i, i ^ mask) for i in range(lax.axis_size(axi...]
    dot_general x90 -> x0, matrix products: 36.7 us -> none  [the longest x60 23.6 us: convolve(): jnp.einsum('tczyx,tco->ozyx', slices_of(padded, plane_shift, row_count),...]
    pallas_call x0 -> x10, Pallas kernels: none -> 17.6 us  [the longest x4 7.41 us: local(): pl.pallas_call(functools.partial(forward_kernel, sizes, skip is not None)...]
    another operation x68 -> x4, local copies, waits for them, and re-layouts: 11.8 us -> 2.38 us  [the longest x2 1.87 us: local(): kernels = weights[0].reshape(2, 3, 3, 3, channels, channels)]
    dynamic_update_slice x36 -> x0, other arithmetic: 4.94 us -> none  [place(): lax.dynamic_update_index_in_dim(buffer, jnp.where(active, value, pick(buf...]
  transfers between devices with their start and end apart: 55 -> 25, of which waited for: 21 -> 12; matrix products, arithmetic and copies ran while one was open for 27% -> 3% of each run, Pallas kernels for 0% -> 4%
where the time goes in v1:
time: 114 us
  starting transfers between devices  64.8 us (57%)
  waiting for transfers between devices  20.6 us (18%)
  Pallas kernels  17.6 us (15%)
  local copies, waits for them, and re-layouts  6.71 us (6%)
  other arithmetic  2.67 us (2%)
  between operations  1.38 us (1%)
    ppermute x8, starting transfers between devices, with_halos(): low = lax.ppermute(block[:, -width:], 'gy', forward)  36 us
    ppermute x6, starting transfers between devices, partner(): lax.ppermute(array, axis, [(i, i ^ mask) for i in range(lax.axis_size(axi...  12.5 us
    ppermute x8, starting transfers between devices, with_halos(): high = lax.ppermute(block[:, :width], 'gy', backward)  10.3 us
    ppermute x6, waiting for transfers between devices, partner(): lax.ppermute(array, axis, [(i, i ^ mask) for i in range(lax.axis_size(axi...  9.87 us
    pallas_call x4, Pallas kernels, local(): pl.pallas_call(functools.partial(forward_kernel, sizes, skip is not None)...  7.41 us
    ppermute x3, waiting for transfers between devices, local(): lax.ppermute(compact, 'segment', [(i, (i + step) % sections) for i in ran...  6.92 us
    ppermute x3, starting transfers between devices, local(): lax.ppermute(compact, 'segment', [(i, (i + step) % sections) for i in ran...  5.97 us
    pallas_call x4, Pallas kernels, local(): pl.pallas_call(functools.partial(backward_kernel, sizes, s < 2, s > 0), o...  5.88 us
  transfers between devices with their start and end apart: 25, of which 12 were waited for; matrix products, arithmetic and copies ran while one was open for 3% of the time, Pallas kernels for 4%

profile of v1, /device:TPU:0, one launch (start us, length us, event | category | flops | bytes accessed | tf_op | source)
XLA Modules:
  0.0 113.8 jit_solution(11350797566113872845)
XLA Ops:
  2.5 1.6 %rev.4 = bf16[2,3,3,3,32,32]{5,2,4,3,1,0:T(4,128)(2,1)S(1)} reverse(bf16[2,3,3,3,32,32]{5,2,4,3,1,0:T(4,128)(2,1)S(1)} %copy.16), dimensions={1,2,3} | reverse | bytes 221184 | tf_op jit(solution)/shard_map/jit(_flip)/rev | solution.py:246
  4.8 3.0 %collective-permute-start.2 = (bf16[2,2,9,32,128]{4,3,2,0,1:T(8,128)(2,1)S(1)}, bf16[2,2,9,32,128]{4,3,2,0,1:T(8,128)(2,1)S(1)}, u32[]{:S(2)}, u32[]{:S(2)}) collective-permute-start(bf16[2,2,9,32,128]{4,3,2,0,1:T(8,128)(2,1)S(1)} %get-tuple-element.107), channel_id=1, source_target_pairs={{0,8},{8,16},{16,24},{24,0},{1,9},{9,17},{17,25},{25,1},{2,10},{10... | collective-permute-start | bytes 884744 | tf_op jit(solution)/shard_map/ppermute | solution.py:252
  7.8 1.5 %collective-permute-start.3 = (bf16[2,2,9,32,128]{4,3,2,0,1:T(8,128)(2,1)S(1)}, bf16[2,2,9,32,128]{4,3,2,0,1:T(8,128)(2,1)S(1)}, u32[]{:S(2)}, u32[]{:S(2)}) collective-permute-start(bf16[2,2,9,32,128]{4,3,2,0,1:T(8,128)(2,1)S(1)} %get-tuple-element.107), channel_id=1, source_target_pairs={{0,16},{8,24},{16,0},{24,8},{1,17},{9,25},{17,1},{25,9},{2,18},{10... | collective-permute-start | bytes 884744 | tf_op jit(solution)/shard_map/ppermute | solution.py:252
  9.3 1.4 %collective-permute-start.4 = (bf16[2,2,9,32,128]{4,3,2,0,1:T(8,128)(2,1)S(1)}, bf16[2,2,9,32,128]{4,3,2,0,1:T(8,128)(2,1)S(1)}, u32[]{:S(2)}, u32[]{:S(2)}) collective-permute-start(bf16[2,2,9,32,128]{4,3,2,0,1:T(8,128)(2,1)S(1)} %get-tuple-element.107), channel_id=1, source_target_pairs={{0,24},{8,0},{16,8},{24,16},{1,25},{9,1},{17,9},{25,17},{2,26},{10... | collective-permute-start | bytes 884744 | tf_op jit(solution)/shard_map/ppermute | solution.py:252
  12.2 3.0 %collective-permute-start = (bf16[4,64,128]{2,1,0:T(8,128)(2,1)S(1)}, bf16[4,64,128]{2,1,0:T(8,128)(2,1)S(1)}, u32[]{:S(2)}, u32[]{:S(2)}) collective-permute-start(bf16[4,64,128]{2,1,0:T(8,128)(2,1)S(1)} %get-tuple-element.123), channel_id=1, source_target_pairs={{0,1},{1,2},{2,3},{3,4},{4,5},{5,6},{6,7},{8,9},{9,10},{10,11},{11... | collective-permute-start | bytes 196616 | tf_op jit(solution)/shard_map/ppermute | solution.py:219
  16.7 5.4 %collective-permute-done.3 = bf16[2,2,9,32,128]{4,3,2,0,1:T(8,128)(2,1)S(1)} collective-permute-done((bf16[2,2,9,32,128]{4,3,2,0,1:T(8,128)(2,1)S(1)}, bf16[2,2,9,32,128]{4,3,2,0,1:T(8,128)(2,1)S(1)}, u32[]{:S(2)}, u32[]{:S(2)}) %collective-permute-start.3) | collective-permute-done | bytes 294944 | tf_op jit(solution)/shard_map/ppermute | solution.py:252
  22.9 1.7 %shard_map.58 = (bf16[4,128,128]{2,1,0:T(8,128)(2,1)S(1)}, bf16[4,128,128]{2,1,0:T(8,128)(2,1)S(1)}, bf16[4,256,128]{2,1,0:T(8,128)(2,1)S(1)}, bf16[4,256,128]{2...) custom-call(bf16[4,64,128]{2,1,0:T(8,128)(2,1)S(1)} %collective-permute-done.low_ref, ...), custom_call_target="tpu_custom_call" | custom-call | tf_op jit(solution)/shard_map/pallas_call | solution.py:281
  25.9 3.0 %collective-permute-start.5 = (bf16[4,64,128]{2,1,0:T(8,128)(2,1)S(1)}, bf16[4,64,128]{2,1,0:T(8,128)(2,1)S(1)}, u32[]{:S(2)}, u32[]{:S(2)}) collective-permute-start(bf16[4,64,128]{2,1,0:T(8,128)(2,1)S(1)} %get-tuple-element.121), channel_id=1, source_target_pairs={{0,1},{1,2},{2,3},{3,4},{4,5},{5,6},{6,7},{8,9},{9,10},{10,11},{11... | collective-permute-start | bytes 196616 | tf_op jit(solution)/shard_map/ppermute | solution.py:219
  29.9 1.7 %shard_map.59 = (bf16[4,128,128]{2,1,0:T(8,128)(2,1)S(1)}, bf16[4,128,128]{2,1,0:T(8,128)(2,1)S(1)}, bf16[4,256,128]{2,1,0:T(8,128)(2,1)S(1)}, bf16[4,256,128]{2...) custom-call(bf16[4,64,128]{2,1,0:T(8,128)(2,1)S(1)} %collective-permute-done.5.low_ref, ...), custom_call_target="tpu_custom_call" | custom-call | tf_op jit(solution)/shard_map/pallas_call | solution.py:281
  32.9 4.2 %collective-permute-start.7 = (bf16[4,64,128]{2,1,0:T(8,128)(2,1)S(1)}, bf16[4,64,128]{2,1,0:T(8,128)(2,1)S(1)}, u32[]{:S(2)}, u32[]{:S(2)}) collective-permute-start(bf16[4,64,128]{2,1,0:T(8,128)(2,1)S(1)} %get-tuple-element.119), channel_id=1, source_target_pairs={{0,1},{1,2},{2,3},{3,4},{4,5},{5,6},{6,7},{8,9},{9,10},{10,11},{11... | collective-permute-start | bytes 196616 | tf_op jit(solution)/shard_map/ppermute | solution.py:219
  37.9 1.7 %shard_map.60 = (bf16[4,128,128]{2,1,0:T(8,128)(2,1)S(1)}, bf16[4,128,128]{2,1,0:T(8,128)(2,1)S(1)}, bf16[4,256,128]{2,1,0:T(8,128)(2,1)S(1)}, bf16[4,256,128]{2...) custom-call(bf16[4,64,128]{2,1,0:T(8,128)(2,1)S(1)} %collective-permute-done.7.low_ref, ...), custom_call_target="tpu_custom_call" | custom-call | tf_op jit(solution)/shard_map/pallas_call | solution.py:281
  40.9 5.3 %collective-permute-start.9 = (bf16[4,64,128]{2,1,0:T(8,128)(2,1)S(1)}, bf16[4,64,128]{2,1,0:T(8,128)(2,1)S(1)}, u32[]{:S(2)}, u32[]{:S(2)}) collective-permute-start(bf16[4,64,128]{2,1,0:T(8,128)(2,1)S(1)} %get-tuple-element.117), channel_id=1, source_target_pairs={{0,1},{1,2},{2,3},{3,4},{4,5},{5,6},{6,7},{8,9},{9,10},{10,11},{11... | collective-permute-start | bytes 196616 | tf_op jit(solution)/shard_map/ppermute | solution.py:219
  47.2 2.4 %shard_map.61 = (bf16[4,128,128]{2,1,0:T(8,128)(2,1)S(1)}, bf16[4,128,128]{2,1,0:T(8,128)(2,1)}, bf16[4,256,128]{2,1,0:T(8,128)(2,1)S(1)}, bf16[4,256,128]{2,1,0...) custom-call(bf16[4,64,128]{2,1,0:T(8,128)(2,1)S(1)} %collective-permute-done.9.low_ref, ...), custom_call_target="tpu_custom_call" | custom-call | tf_op jit(solution)/shard_map/pallas_call | solution.py:281
  50.9 5.3 %collective-permute-start.12 = (bf16[4,64,128]{2,1,0:T(8,128)(2,1)S(1)}, bf16[4,64,128]{2,1,0:T(8,128)(2,1)S(1)}, u32[]{:S(2)}, u32[]{:S(2)}) collective-permute-start(bf16[4,64,128]{2,1,0:T(8,128)(2,1)S(1)} %get-tuple-element.115), channel_id=1, source_target_pairs={{0,1},{1,2},{2,3},{3,4},{4,5},{5,6},{6,7},{8,9},{9,10},{10,11},{11... | collective-permute-start | bytes 196616 | tf_op jit(solution)/shard_map/ppermute | solution.py:219
  56.2 1.8 %collective-permute-start.11 = (bf16[4,128,128]{2,1,0:T(8,128)(2,1)S(1)}, bf16[4,128,128]{2,1,0:T(8,128)(2,1)S(1)}, u32[]{:S(2)}, u32[]{:S(2)}) collective-permute-start(bf16[4,128,128]{2,1,0:T(8,128)(2,1)S(1)} %get-tuple-element.79), channel_id=1, source_target_pairs={{0,8},{8,0},{16,24},{24,16},{1,9},{9,1},{17,25},{25,17},{2,10},{10... | collective-permute-start | bytes 393224 | tf_op jit(solution)/shard_map/ppermute | solution.py:225
  58.1 1.5 %shard_map.62 = (bf16[4,128,128]{2,1,0:T(8,128)(2,1)S(1)}, bf16[4,128,128]{2,1,0:T(8,128)(2,1)S(1)}, bf16[4,128,128]{2,1,0:T(8,128)(2,1)S(1)}) custom-call(bf16[4,64,128]{2,1,0:T(8,128)(2,1)S(1)} %collective-permute-done.12.low_ref, bf16[4,128,128]{2,1,0:T(8,128)(2,1)S(1)} %fusion.3.mid_ref, bf16[4,64,128]{2,1,0:T(8,128)(2,1)S(1)} %collective-permute-done.13.high_ref, ...), custom_call_target="tpu_custom_call" | custom-call | tf_op jit(solution)/shard_map/pallas_call | solution.py:320
  60.9 4.6 %collective-permute-start.14 = (bf16[4,64,128]{2,1,0:T(8,128)(2,1)S(1)}, bf16[4,64,128]{2,1,0:T(8,128)(2,1)S(1)}, u32[]{:S(2)}, u32[]{:S(2)}) collective-permute-start(bf16[4,64,128]{2,1,0:T(8,128)(2,1)S(1)} %get-tuple-element.113), channel_id=1, source_target_pairs={{0,1},{1,2},{2,3},{3,4},{4,5},{5,6},{6,7},{8,9},{9,10},{10,11},{11... | collective-permute-start | bytes 196616 | tf_op jit(solution)/shard_map/ppermute | solution.py:219
  66.4 1.5 %shard_map.63 = (bf16[4,128,128]{2,1,0:T(8,128)(2,1)S(1)}, bf16[4,128,128]{2,1,0:T(8,128)(2,1)S(1)}, bf16[4,128,128]{2,1,0:T(8,128)(2,1)S(1)}) custom-call(bf16[4,64,128]{2,1,0:T(8,128)(2,1)S(1)} %collective-permute-done.14.low_ref, bf16[4,128,128]{2,1,0:T(8,128)(2,1)S(1)} %get-tuple-element.49.mid_ref, ...), custom_call_target="tpu_custom_call" | custom-call | tf_op jit(solution)/shard_map/pallas_call | solution.py:320
  69.2 5.2 %collective-permute-start.16 = (bf16[4,64,128]{2,1,0:T(8,128)(2,1)S(1)}, bf16[4,64,128]{2,1,0:T(8,128)(2,1)S(1)}, u32[]{:S(2)}, u32[]{:S(2)}) collective-permute-start(bf16[4,64,128]{2,1,0:T(8,128)(2,1)S(1)} %get-tuple-element.111), channel_id=1, source_target_pairs={{0,1},{1,2},{2,3},{3,4},{4,5},{5,6},{6,7},{8,9},{9,10},{10,11},{11... | collective-permute-start | bytes 196616 | tf_op jit(solution)/shard_map/ppermute | solution.py:219
  75.1 1.5 %shard_map.64 = (bf16[4,128,128]{2,1,0:T(8,128)(2,1)S(1)}, bf16[4,128,128]{2,1,0:T(8,128)(2,1)S(1)}, bf16[4,128,128]{2,1,0:T(8,128)(2,1)S(1)}) custom-call(bf16[4,64,128]{2,1,0:T(8,128)(2,1)S(1)} %collective-permute-done.16.low_ref, bf16[4,128,128]{2,1,0:T(8,128)(2,1)S(1)} %get-tuple-element.53.mid_ref, ...), custom_call_target="tpu_custom_call" | custom-call | tf_op jit(solution)/shard_map/pallas_call | solution.py:320
  77.9 5.3 %collective-permute-start.18 = (bf16[4,64,128]{2,1,0:T(8,128)(2,1)S(1)}, bf16[4,64,128]{2,1,0:T(8,128)(2,1)S(1)}, u32[]{:S(2)}, u32[]{:S(2)}) collective-permute-start(bf16[4,64,128]{2,1,0:T(8,128)(2,1)S(1)} %get-tuple-element.109), channel_id=1, source_target_pairs={{0,1},{1,2},{2,3},{3,4},{4,5},{5,6},{6,7},{8,9},{9,10},{10,11},{11... | collective-permute-start | bytes 196616 | tf_op jit(solution)/shard_map/ppermute | solution.py:219
  83.3 2.1 %shard_map.67 = f32[2,32,864]{2,1,0:T(8,128)S(1)} custom-call(bf16[4,256,128]{2,1,0:T(8,128)(2,1)S(1)} %broadcast_select_fusion.1.frame_ref, bf16[4,128,128]{2,1,0:T(8,128)(2,1)S(1)} %broadcast_select_fusion.7.first_ref, bf16[4,256,128]{2,1,0:T(8,128)(2,1)S(1)} %broadcast_select_fusion.hidden_ref, bf16[4,128,128]{2,1,0:T(8,128)(2,1)S(1)} %broadcast_select_fusion.6.second_ref), custom_call_target="tpu_custom_call" | custom-call | tf_op jit(solution)/shard_map/pallas_call | solution.py:350
  85.5 1.5 %shard_map.65 = (bf16[4,128,128]{2,1,0:T(8,128)(2,1)S(1)}, bf16[4,128,128]{2,1,0:T(8,128)(2,1)S(1)}) custom-call(bf16[4,64,128]{2,1,0:T(8,128)(2,1)S(1)} %collective-permute-done.18.low_ref, bf16[4,128,128]{2,1,0:T(8,128)(2,1)S(1)} %get-tuple-element.57.mid_ref, bf16[4,64,128]{2,1,0:T(8,128)(2,1)S(1)} %collective-permute-done.19.high_ref, ...), custom_call_target="tpu_custom_call" | custom-call | tf_op jit(solution)/shard_map/pallas_call | solution.py:320
  87.0 2.1 %shard_map.66 = f32[2,32,864]{2,1,0:T(8,128)S(1)} custom-call(bf16[4,256,128]{2,1,0:T(8,128)(2,1)S(1)} %broadcast_select_fusion.3.frame_ref, bf16[4,128,128]{2,1,0:T(8,128)(2,1)S(1)} %broadcast_select_fusion.9.first_ref, bf16[4,256,128]{2,1,0:T(8,128)(2,1)S(1)} %broadcast_select_fusion.2.hidden_ref, bf16[4,128,128]{2,1,0:T(8,128)(2,1)S(1)} %broadcast_select_fusion.8.second_ref), custom_call_target="tpu_custom_call" | custom-call | tf_op jit(solution)/shard_map/pallas_call | solution.py:350
  89.2 1.8 %collective-permute-start.20 = (bf16[2,32,864]{2,1,0:T(8,128)(2,1)S(1)}, bf16[2,32,864]{2,1,0:T(8,128)(2,1)S(1)}, u32[]{:S(2)}, u32[]{:S(2)}) collective-permute-start(bf16[2,32,864]{2,1,0:T(8,128)(2,1)S(1)} %select_convert_fusion), channel_id=1, source_target_pairs={{0,8},{8,0},{16,24},{24,16},{1,9},{9,1},{17,25},{25,17},{2,10},{10... | collective-permute-start | bytes 331784 | tf_op jit(solution)/shard_map/ppermute | solution.py:225
  91.8 2.2 %collective-permute-done.20 = bf16[2,32,864]{2,1,0:T(8,128)(2,1)S(1)} collective-permute-done((bf16[2,32,864]{2,1,0:T(8,128)(2,1)S(1)}, bf16[2,32,864]{2,1,0:T(8,128)(2,1)S(1)}, u32[]{:S(2)}, u32[]{:S(2)}) %collective-permute-start.20) | collective-permute-done | bytes 110624 | tf_op jit(solution)/shard_map/ppermute | solution.py:225
  95.4 1.8 %collective-permute-start.24 = (bf16[4,128,128]{2,1,0:T(8,128)(2,1)S(1)}, bf16[4,128,128]{2,1,0:T(8,128)(2,1)S(1)}, u32[]{:S(2)}, u32[]{:S(2)}) collective-permute-start(bf16[4,128,128]{2,1,0:T(8,128)(2,1)S(1)} %get-tuple-element.74), channel_id=1, source_target_pairs={{0,8},{8,0},{16,24},{24,16},{1,9},{9,1},{17,25},{25,17},{2,10},{10... | collective-permute-start | bytes 393224 | tf_op jit(solution)/shard_map/ppermute | solution.py:225
  97.2 3.1 %collective-permute-start.22 = (bf16[2,32,864]{2,1,0:T(8,128)(2,1)S(1)}, bf16[2,32,864]{2,1,0:T(8,128)(2,1)S(1)}, u32[]{:S(2)}, u32[]{:S(2)}) collective-permute-start(bf16[2,32,864]{2,1,0:T(8,128)(2,1)S(1)} %fusion.4), channel_id=1, source_target_pairs={{0,2},{1,3},{2,0},{3,1},{4,6},{5,7},{6,4},{7,5},{8,10},{9,11},{10,... | collective-permute-start | bytes 331784 | tf_op jit(solution)/shard_map/ppermute | solution.py:225
  101.0 2.7 %collective-permute-done.22 = bf16[2,32,864]{2,1,0:T(8,128)(2,1)S(1)} collective-permute-done((bf16[2,32,864]{2,1,0:T(8,128)(2,1)S(1)}, bf16[2,32,864]{2,1,0:T(8,128)(2,1)S(1)}, u32[]{:S(2)}, u32[]{:S(2)}) %collective-permute-start.22) | collective-permute-done | bytes 110624 | tf_op jit(solution)/shard_map/ppermute | solution.py:225
  103.8 2.8 %collective-permute-start.23 = (bf16[2,32,864]{2,1,0:T(8,128)(2,1)S(1)}, bf16[2,32,864]{2,1,0:T(8,128)(2,1)S(1)}, u32[]{:S(2)}, u32[]{:S(2)}) collective-permute-start(bf16[2,32,864]{2,1,0:T(8,128)(2,1)S(1)} %fusion.5), channel_id=1, source_target_pairs={{0,4},{1,5},{2,6},{3,7},{4,0},{5,1},{6,2},{7,3},{8,12},{9,13},{10,... | collective-permute-start | bytes 331784 | tf_op jit(solution)/shard_map/ppermute | solution.py:225
  107.6 4.3 %collective-permute-done.23 = bf16[2,32,864]{2,1,0:T(8,128)(2,1)S(1)} collective-permute-done((bf16[2,32,864]{2,1,0:T(8,128)(2,1)S(1)}, bf16[2,32,864]{2,1,0:T(8,128)(2,1)S(1)}, u32[]{:S(2)}, u32[]{:S(2)}) %collective-permute-start.23) | collective-permute-done | bytes 110624 | tf_op jit(solution)/shard_map/ppermute | solution.py:225
  112.4 1.4 %copy.26 = f32[1,2,27,32,32]{4,3,2,1,0:T(8,128)} copy(f32[1,2,27,32,32]{3,2,4,1,0:T(8,128)S(1)} %bitcast.94) | data formatting | bytes 442368
  (86 shorter events, 24.0 us)
Async XLA Ops:
  0.6 10.1 %copy-start = (bf16[2,32,4,4,128]{4,3,2,1,0:T(4,128)(2,1)S(1)}, bf16[2,32,4,4,128]{4,3,2,1,0:T(4,128)(2,1)}, u32[]{:S(2)}) copy-start(bf16[2,32,4,4,128]{4,3,2,1,0:T(4,128)(2,1)} %param.3) | copy-start | bytes 786436
  0.6 1.4 %copy-start.1 = (bf16[1,2,27,32,32]{4,3,2,1,0:T(8,128)(2,1)S(1)}, bf16[1,2,27,32,32]{4,3,2,1,0:T(8,128)(2,1)}, u32[]{:S(2)}) copy-start(bf16[1,2,27,32,32]{4,3,2,1,0:T(8,128)(2,1)} %param.5) | copy-start | bytes 331780
  4.4 10.9 %copy-start.2 = (bf16[2,32,4,4,128]{4,3,2,1,0:T(4,128)(2,1)S(1)}, bf16[2,32,4,4,128]{4,3,2,1,0:T(4,128)(2,1)}, u32[]{:S(2)}) copy-start(bf16[2,32,4,4,128]{4,3,2,1,0:T(4,128)(2,1)} %param.4) | copy-start | bytes 786436
  4.8 11.9 %collective-permute-start.2 = (bf16[2,2,9,32,128]{4,3,2,0,1:T(8,128)(2,1)S(1)}, bf16[2,2,9,32,128]{4,3,2,0,1:T(8,128)(2,1)S(1)}, u32[]{:S(2)}, u32[]{:S(2)}) collective-permute-start(bf16[2,2,9,32,128]{4,3,2,0,1:T(8,128)(2,1)S(1)} %get-tuple-element.107), channel_id=1, source_target_pairs={{0,8},{8,16},{16,24},{24,0},{1,9},{9,17},{17,25},{25,1},{2,10},{10... | collective-permute-start | bytes 884744 | tf_op jit(solution)/shard_map/ppermute | solution.py:252
  7.8 14.3 %collective-permute-start.3 = (bf16[2,2,9,32,128]{4,3,2,0,1:T(8,128)(2,1)S(1)}, bf16[2,2,9,32,128]{4,3,2,0,1:T(8,128)(2,1)S(1)}, u32[]{:S(2)}, u32[]{:S(2)}) collective-permute-start(bf16[2,2,9,32,128]{4,3,2,0,1:T(8,128)(2,1)S(1)} %get-tuple-element.107), channel_id=1, source_target_pairs={{0,16},{8,24},{16,0},{24,8},{1,17},{9,25},{17,1},{25,9},{2,18},{10... | collective-permute-start | bytes 884744 | tf_op jit(solution)/shard_map/ppermute | solution.py:252
  9.3 13.1 %collective-permute-start.4 = (bf16[2,2,9,32,128]{4,3,2,0,1:T(8,128)(2,1)S(1)}, bf16[2,2,9,32,128]{4,3,2,0,1:T(8,128)(2,1)S(1)}, u32[]{:S(2)}, u32[]{:S(2)}) collective-permute-start(bf16[2,2,9,32,128]{4,3,2,0,1:T(8,128)(2,1)S(1)} %get-tuple-element.107), channel_id=1, source_target_pairs={{0,24},{8,0},{16,8},{24,16},{1,25},{9,1},{17,9},{25,17},{2,26},{10... | collective-permute-start | bytes 884744 | tf_op jit(solution)/shard_map/ppermute | solution.py:252
  10.9 12.1 %collective-permute-start.1 = (bf16[4,64,128]{2,1,0:T(8,128)(2,1)S(1)}, bf16[4,64,128]{2,1,0:T(8,128)(2,1)S(1)}, u32[]{:S(2)}, u32[]{:S(2)}) collective-permute-start(bf16[4,64,128]{2,1,0:T(8,128)(2,1)S(1)} %get-tuple-element.122), channel_id=1, source_target_pairs={{1,0},{2,1},{3,2},{4,3},{5,4},{6,5},{7,6},{9,8},{10,9},{11,10},{12... | collective-permute-start | bytes 196616 | tf_op jit(solution)/shard_map/ppermute | solution.py:220
  12.2 10.8 %collective-permute-start = (bf16[4,64,128]{2,1,0:T(8,128)(2,1)S(1)}, bf16[4,64,128]{2,1,0:T(8,128)(2,1)S(1)}, u32[]{:S(2)}, u32[]{:S(2)}) collective-permute-start(bf16[4,64,128]{2,1,0:T(8,128)(2,1)S(1)} %get-tuple-element.123), channel_id=1, source_target_pairs={{0,1},{1,2},{2,3},{3,4},{4,5},{5,6},{6,7},{8,9},{9,10},{10,11},{11... | collective-permute-start | bytes 196616 | tf_op jit(solution)/shard_map/ppermute | solution.py:219
  24.6 4.4 %collective-permute-start.6 = (bf16[4,64,128]{2,1,0:T(8,128)(2,1)S(1)}, bf16[4,64,128]{2,1,0:T(8,128)(2,1)S(1)}, u32[]{:S(2)}, u32[]{:S(2)}) collective-permute-start(bf16[4,64,128]{2,1,0:T(8,128)(2,1)S(1)} %get-tuple-element.120), channel_id=1, source_target_pairs={{1,0},{2,1},{3,2},{4,3},{5,4},{6,5},{7,6},{9,8},{10,9},{11,10},{12... | collective-permute-start | bytes 196616 | tf_op jit(solution)/shard_map/ppermute | solution.py:220
  25.9 3.9 %collective-permute-start.5 = (bf16[4,64,128]{2,1,0:T(8,128)(2,1)S(1)}, bf16[4,64,128]{2,1,0:T(8,128)(2,1)S(1)}, u32[]{:S(2)}, u32[]{:S(2)}) collective-permute-start(bf16[4,64,128]{2,1,0:T(8,128)(2,1)S(1)} %get-tuple-element.121), channel_id=1, source_target_pairs={{0,1},{1,2},{2,3},{3,4},{4,5},{5,6},{6,7},{8,9},{9,10},{10,11},{11... | collective-permute-start | bytes 196616 | tf_op jit(solution)/shard_map/ppermute | solution.py:219
  31.6 5.5 %collective-permute-start.8 = (bf16[4,64,128]{2,1,0:T(8,128)(2,1)S(1)}, bf16[4,64,128]{2,1,0:T(8,128)(2,1)S(1)}, u32[]{:S(2)}, u32[]{:S(2)}) collective-permute-start(bf16[4,64,128]{2,1,0:T(8,128)(2,1)S(1)} %get-tuple-element.118), channel_id=1, source_target_pairs={{1,0},{2,1},{3,2},{4,3},{5,4},{6,5},{7,6},{9,8},{10,9},{11,10},{12... | collective-permute-start | bytes 196616 | tf_op jit(solution)/shard_map/ppermute | solution.py:220
  32.9 5.0 %collective-permute-start.7 = (bf16[4,64,128]{2,1,0:T(8,128)(2,1)S(1)}, bf16[4,64,128]{2,1,0:T(8,128)(2,1)S(1)}, u32[]{:S(2)}, u32[]{:S(2)}) collective-permute-start(bf16[4,64,128]{2,1,0:T(8,128)(2,1)S(1)} %get-tuple-element.119), channel_id=1, source_target_pairs={{0,1},{1,2},{2,3},{3,4},{4,5},{5,6},{6,7},{8,9},{9,10},{10,11},{11... | collective-permute-start | bytes 196616 | tf_op jit(solution)/shard_map/ppermute | solution.py:219
  39.6 6.7 %collective-permute-start.10 = (bf16[4,64,128]{2,1,0:T(8,128)(2,1)S(1)}, bf16[4,64,128]{2,1,0:T(8,128)(2,1)S(1)}, u32[]{:S(2)}, u32[]{:S(2)}) collective-permute-start(bf16[4,64,128]{2,1,0:T(8,128)(2,1)S(1)} %get-tuple-element.116), channel_id=1, source_target_pairs={{1,0},{2,1},{3,2},{4,3},{5,4},{6,5},{7,6},{9,8},{10,9},{11,10},{12... | collective-permute-start | bytes 196616 | tf_op jit(solution)/shard_map/ppermute | solution.py:220
  40.9 6.2 %collective-permute-start.9 = (bf16[4,64,128]{2,1,0:T(8,128)(2,1)S(1)}, bf16[4,64,128]{2,1,0:T(8,128)(2,1)S(1)}, u32[]{:S(2)}, u32[]{:S(2)}) collective-permute-start(bf16[4,64,128]{2,1,0:T(8,128)(2,1)S(1)} %get-tuple-element.117), channel_id=1, source_target_pairs={{0,1},{1,2},{2,3},{3,4},{4,5},{5,6},{6,7},{8,9},{9,10},{10,11},{11... | collective-permute-start | bytes 196616 | tf_op jit(solution)/shard_map/ppermute | solution.py:219
  49.6 8.5 %collective-permute-start.13 = (bf16[4,64,128]{2,1,0:T(8,128)(2,1)S(1)}, bf16[4,64,128]{2,1,0:T(8,128)(2,1)S(1)}, u32[]{:S(2)}, u32[]{:S(2)}) collective-permute-start(bf16[4,64,128]{2,1,0:T(8,128)(2,1)S(1)} %get-tuple-element.114), channel_id=1, source_target_pairs={{1,0},{2,1},{3,2},{4,3},{5,4},{6,5},{7,6},{9,8},{10,9},{11,10},{12... | collective-permute-start | bytes 196616 | tf_op jit(solution)/shard_map/ppermute | solution.py:220
  50.9 7.2 %collective-permute-start.12 = (bf16[4,64,128]{2,1,0:T(8,128)(2,1)S(1)}, bf16[4,64,128]{2,1,0:T(8,128)(2,1)S(1)}, u32[]{:S(2)}, u32[]{:S(2)}) collective-permute-start(bf16[4,64,128]{2,1,0:T(8,128)(2,1)S(1)} %get-tuple-element.115), channel_id=1, source_target_pairs={{0,1},{1,2},{2,3},{3,4},{4,5},{5,6},{6,7},{8,9},{9,10},{10,11},{11... | collective-permute-start | bytes 196616 | tf_op jit(solution)/shard_map/ppermute | solution.py:219
  56.2 18.2 %collective-permute-start.11 = (bf16[4,128,128]{2,1,0:T(8,128)(2,1)S(1)}, bf16[4,128,128]{2,1,0:T(8,128)(2,1)S(1)}, u32[]{:S(2)}, u32[]{:S(2)}) collective-permute-start(bf16[4,128,128]{2,1,0:T(8,128)(2,1)S(1)} %get-tuple-element.79), channel_id=1, source_target_pairs={{0,8},{8,0},{16,24},{24,16},{1,9},{9,1},{17,25},{25,17},{2,10},{10... | collective-permute-start | bytes 393224 | tf_op jit(solution)/shard_map/ppermute | solution.py:225
  59.6 6.0 %collective-permute-start.15 = (bf16[4,64,128]{2,1,0:T(8,128)(2,1)S(1)}, bf16[4,64,128]{2,1,0:T(8,128)(2,1)S(1)}, u32[]{:S(2)}, u32[]{:S(2)}) collective-permute-start(bf16[4,64,128]{2,1,0:T(8,128)(2,1)S(1)} %get-tuple-element.112), channel_id=1, source_target_pairs={{1,0},{2,1},{3,2},{4,3},{5,4},{6,5},{7,6},{9,8},{10,9},{11,10},{12... | collective-permute-start | bytes 196616 | tf_op jit(solution)/shard_map/ppermute | solution.py:220
  60.9 5.5 %collective-permute-start.14 = (bf16[4,64,128]{2,1,0:T(8,128)(2,1)S(1)}, bf16[4,64,128]{2,1,0:T(8,128)(2,1)S(1)}, u32[]{:S(2)}, u32[]{:S(2)}) collective-permute-start(bf16[4,64,128]{2,1,0:T(8,128)(2,1)S(1)} %get-tuple-element.113), channel_id=1, source_target_pairs={{0,1},{1,2},{2,3},{3,4},{4,5},{5,6},{6,7},{8,9},{9,10},{10,11},{11... | collective-permute-start | bytes 196616 | tf_op jit(solution)/shard_map/ppermute | solution.py:219
  67.9 6.8 %collective-permute-start.17 = (bf16[4,64,128]{2,1,0:T(8,128)(2,1)S(1)}, bf16[4,64,128]{2,1,0:T(8,128)(2,1)S(1)}, u32[]{:S(2)}, u32[]{:S(2)}) collective-permute-start(bf16[4,64,128]{2,1,0:T(8,128)(2,1)S(1)} %get-tuple-element.110), channel_id=1, source_target_pairs={{1,0},{2,1},{3,2},{4,3},{5,4},{6,5},{7,6},{9,8},{10,9},{11,10},{12... | collective-permute-start | bytes 196616 | tf_op jit(solution)/shard_map/ppermute | solution.py:220
  69.2 5.9 %collective-permute-start.16 = (bf16[4,64,128]{2,1,0:T(8,128)(2,1)S(1)}, bf16[4,64,128]{2,1,0:T(8,128)(2,1)S(1)}, u32[]{:S(2)}, u32[]{:S(2)}) collective-permute-start(bf16[4,64,128]{2,1,0:T(8,128)(2,1)S(1)} %get-tuple-element.111), channel_id=1, source_target_pairs={{0,1},{1,2},{2,3},{3,4},{4,5},{5,6},{6,7},{8,9},{9,10},{10,11},{11... | collective-permute-start | bytes 196616 | tf_op jit(solution)/shard_map/ppermute | solution.py:219
  76.6 8.8 %collective-permute-start.19 = (bf16[4,64,128]{2,1,0:T(8,128)(2,1)S(1)}, bf16[4,64,128]{2,1,0:T(8,128)(2,1)S(1)}, u32[]{:S(2)}, u32[]{:S(2)}) collective-permute-start(bf16[4,64,128]{2,1,0:T(8,128)(2,1)S(1)} %get-tuple-element.108), channel_id=1, source_target_pairs={{1,0},{2,1},{3,2},{4,3},{5,4},{6,5},{7,6},{9,8},{10,9},{11,10},{12... | collective-permute-start | bytes 196616 | tf_op jit(solution)/shard_map/ppermute | solution.py:220
  77.9 7.5 %collective-permute-start.18 = (bf16[4,64,128]{2,1,0:T(8,128)(2,1)S(1)}, bf16[4,64,128]{2,1,0:T(8,128)(2,1)S(1)}, u32[]{:S(2)}, u32[]{:S(2)}) collective-permute-start(bf16[4,64,128]{2,1,0:T(8,128)(2,1)S(1)} %get-tuple-element.109), channel_id=1, source_target_pairs={{0,1},{1,2},{2,3},{3,4},{4,5},{5,6},{6,7},{8,9},{9,10},{10,11},{11... | collective-permute-start | bytes 196616 | tf_op jit(solution)/shard_map/ppermute | solution.py:219
  89.2 4.9 %collective-permute-start.20 = (bf16[2,32,864]{2,1,0:T(8,128)(2,1)S(1)}, bf16[2,32,864]{2,1,0:T(8,128)(2,1)S(1)}, u32[]{:S(2)}, u32[]{:S(2)}) collective-permute-start(bf16[2,32,864]{2,1,0:T(8,128)(2,1)S(1)} %select_convert_fusion), channel_id=1, source_target_pairs={{0,8},{8,0},{16,24},{24,16},{1,9},{9,1},{17,25},{25,17},{2,10},{10... | collective-permute-start | bytes 331784 | tf_op jit(solution)/shard_map/ppermute | solution.py:225
  94.1 3.1 %collective-permute-start.21 = (bf16[2,32,864]{2,1,0:T(8,128)(2,1)S(1)}, bf16[2,32,864]{2,1,0:T(8,128)(2,1)S(1)}, u32[]{:S(2)}, u32[]{:S(2)}) collective-permute-start(bf16[2,32,864]{2,1,0:T(8,128)(2,1)S(1)} %get-tuple-element.77), channel_id=1, source_target_pairs={{0,1},{1,0},{2,3},{3,2},{4,5},{5,4},{6,7},{7,6},{8,9},{9,8},{10,11... | collective-permute-start | bytes 331784 | tf_op jit(solution)/shard_map/ppermute | solution.py:225
  95.4 5.5 %collective-permute-start.24 = (bf16[4,128,128]{2,1,0:T(8,128)(2,1)S(1)}, bf16[4,128,128]{2,1,0:T(8,128)(2,1)S(1)}, u32[]{:S(2)}, u32[]{:S(2)}) collective-permute-start(bf16[4,128,128]{2,1,0:T(8,128)(2,1)S(1)} %get-tuple-element.74), channel_id=1, source_target_pairs={{0,8},{8,0},{16,24},{24,16},{1,9},{9,1},{17,25},{25,17},{2,10},{10... | collective-permute-start | bytes 393224 | tf_op jit(solution)/shard_map/ppermute | solution.py:225
  97.2 6.6 %collective-permute-start.22 = (bf16[2,32,864]{2,1,0:T(8,128)(2,1)S(1)}, bf16[2,32,864]{2,1,0:T(8,128)(2,1)S(1)}, u32[]{:S(2)}, u32[]{:S(2)}) collective-permute-start(bf16[2,32,864]{2,1,0:T(8,128)(2,1)S(1)} %fusion.4), channel_id=1, source_target_pairs={{0,2},{1,3},{2,0},{3,1},{4,6},{5,7},{6,4},{7,5},{8,10},{9,11},{10,... | collective-permute-start | bytes 331784 | tf_op jit(solution)/shard_map/ppermute | solution.py:225
  103.8 8.1 %collective-permute-start.23 = (bf16[2,32,864]{2,1,0:T(8,128)(2,1)S(1)}, bf16[2,32,864]{2,1,0:T(8,128)(2,1)S(1)}, u32[]{:S(2)}, u32[]{:S(2)}) collective-permute-start(bf16[2,32,864]{2,1,0:T(8,128)(2,1)S(1)} %fusion.5), channel_id=1, source_target_pairs={{0,4},{1,5},{2,6},{3,7},{4,0},{5,1},{6,2},{7,3},{8,12},{9,13},{10,... | collective-permute-start | bytes 331784 | tf_op jit(solution)/shard_map/ppermute | solution.py:225

commit v2 on v1

--- a/solution.py
+++ b/solution.py
@@ -82,9 +82,9 @@
     inside_low = jnp.where(gy == 0, HALO, 0)
     inside_high = jnp.where(gy == count - 1, rows + HALO, rows + 2 * HALO)
     for z in range(planes):
-        frame_ref[z, : HALO * channels] = low_ref[z]
+        frame_ref[z, : HALO * channels] = jnp.where(gy == 0, 0.0, low_ref[z].astype(jnp.float32)).astype(jnp.bfloat16)
         frame_ref[z, HALO * channels : (HALO + rows) * channels] = mid_ref[z]
-        frame_ref[z, (HALO + rows) * channels :] = high_ref[z]
+        frame_ref[z, (HALO + rows) * channels :] = jnp.where(gy == count - 1, 0.0, high_ref[z].astype(jnp.float32)).astype(jnp.bfloat16)
     fill_columns(col, lambda z: frame_ref[z].astype(jnp.float32), planes)
     build_taps(taps, first_ref, inner)
     mask = row_mask(channels, inner, 1, inside_low, inside_high, across)
@@ -136,9 +136,9 @@
     inside_low = jnp.where(gy == 0, HALO, 0)
     inside_high = jnp.where(gy == count - 1, rows + HALO, rows + 2 * HALO)
     for z in range(planes):
-        wide[z, : HALO * channels] = low_ref[z]
+        wide[z, : HALO * channels] = jnp.where(gy == 0, 0.0, low_ref[z].astype(jnp.float32)).astype(jnp.bfloat16)
         wide[z, HALO * channels : (HALO + rows) * channels] = mid_ref[z]
-        wide[z, (HALO + rows) * channels :] = high_ref[z]
+        wide[z, (HALO + rows) * channels :] = jnp.where(gy == count - 1, 0.0, high_ref[z].astype(jnp.float32)).astype(jnp.bfloat16)
     fill_columns(col, lambda z: wide[z].astype(jnp.float32), planes)
     build_taps(taps, second_ref, inner)
     mask = row_mask(channels, inner, 1, inside_low, inside_high, across)
@@ -211,13 +211,49 @@
         )
 
 
+def exchange_kernel(block_ref, low_ref, high_ref, send_sem, recv_sem):
+    count = lax.axis_size("gy")
+    me = lax.axis_index("gy")
+    after, before = lax.rem(me + 1, count), lax.rem(me + count - 1, count)
+    barrier = pltpu.get_barrier_semaphore()
+    for neighbour in (before, after):
+        pl.semaphore_signal(
+            barrier, inc=1, device_id={"gy": neighbour}, device_id_type=pl.DeviceIdType.MESH
+        )
+    pl.semaphore_wait(barrier, 2)
+    width = low_ref.shape[1]
+    last = block_ref.shape[1] - width
+    copies = [
+        pltpu.make_async_remote_copy(
+            src_ref=block_ref.at[:, pl.ds(start, width), :],
+            dst_ref=target,
+            send_sem=send_sem.at[k],
+            recv_sem=recv_sem.at[k],
+            device_id={"gy": neighbour},
+            device_id_type=pl.DeviceIdType.MESH,
+        )
+        for k, (start, target, neighbour) in enumerate(
+            ((last, low_ref, after), (0, high_ref, before))
+        )
+    ]
+    for copy in copies:
+        copy.start()
+    for copy in copies:
+        copy.wait()
+
+
 def with_halos(block, channels):
-    count = lax.axis_size("gy")
     width = HALO * channels
-    forward = [(i, i + 1) for i in range(count - 1)]
-    backward = [(i + 1, i) for i in range(count - 1)]
-    low = lax.ppermute(block[:, -width:], "gy", forward)
-    high = lax.ppermute(block[:, :width], "gy", backward)
+    halo = jax.ShapeDtypeStruct((block.shape[0], width, block.shape[2]), block.dtype)
+    spec = pl.BlockSpec(memory_space=pltpu.VMEM)
+    low, high = pl.pallas_call(
+        exchange_kernel,
+        out_shape=(halo, halo),
+        in_specs=[spec],
+        out_specs=(spec, spec),
+        scratch_shapes=[pltpu.SemaphoreType.DMA((2,)), pltpu.SemaphoreType.DMA((2,))],
+        compiler_params=pltpu.CompilerParams(collective_id=0, has_side_effects=True),
+    )(block)
     return low, block, high
 
 

time: 114 us -> 151 us (1.32)
  Pallas kernels: 17.6 us -> 76.4 us
  starting transfers between devices: 64.8 us -> 9.84 us
  local copies, waits for them, and re-layouts: 6.71 us -> 40.2 us
  waiting for transfers between devices: 20.6 us -> 16.3 us
  other arithmetic: 2.67 us -> 5.27 us
    pallas_call x0 -> x8, Pallas kernels: none -> 58.5 us  [with_halos(): pl.pallas_call(exchange_kernel, out_shape=(halo, halo), in_specs=[spec],...]
    ppermute x16 -> x0, starting transfers between devices: 46.4 us -> none  [the longest x8 36 us: with_halos(): low = lax.ppermute(block[:, -width:], 'gy', forward)]
    unnamed x8 -> x132, local copies, waits for them, and re-layouts: 1.47 us -> 34.3 us
    ppermute x6, starting transfers between devices: 12.5 us -> 3.86 us  [partner(): lax.ppermute(array, axis, [(i, i ^ mask) for i in range(lax.axis_size(axi...]
    ppermute x3, waiting for transfers between devices: 6.92 us -> 2.26 us  [local(): lax.ppermute(compact, 'segment', [(i, (i + step) % sections) for i in ran...]
    ppermute x6, waiting for transfers between devices: 9.87 us -> 14 us  [partner(): lax.ppermute(array, axis, [(i, i ^ mask) for i in range(lax.axis_size(axi...]
    ppermute x16 -> x0, waiting for transfers between devices: 3.83 us -> none  [the longest x8 3.81 us: with_halos(): low = lax.ppermute(block[:, -width:], 'gy', forward)]
    convert_element_type x2, other arithmetic: 0.06 us -> 1.71 us  [local(): second = (outgoing.astype(jnp.float32) * slopes2[-1]).astype(jnp.bfloat16)]
  transfers between devices with their start and end apart: 25 -> 9, of which waited for: 12 -> 7; matrix products, arithmetic and copies ran while one was open for 3% -> 3% of each run, Pallas kernels for 4% -> 5%
where the time goes in v2:
time: 151 us; the launch traced here: 149 us
  Pallas kernels  76.4 us (51%)
  local copies, waits for them, and re-layouts  40.2 us (27%)
  waiting for transfers between devices  16.3 us (11%)
  starting transfers between devices  9.84 us (7%)
  other arithmetic  5.27 us (3%)
    pallas_call x8, Pallas kernels, with_halos(): pl.pallas_call(exchange_kernel, out_shape=(halo, halo), in_specs=[spec],...  58.5 us
    unnamed x132, local copies, waits for them, and re-layouts  34.3 us
    ppermute x6, waiting for transfers between devices, partner(): lax.ppermute(array, axis, [(i, i ^ mask) for i in range(lax.axis_size(axi...  14 us
    pallas_call x4, Pallas kernels, local(): pl.pallas_call(functools.partial(forward_kernel, sizes, skip is not None)...  7.47 us
    pallas_call x4, Pallas kernels, local(): pl.pallas_call(functools.partial(backward_kernel, sizes, s < 2, s > 0), o...  6.16 us
    ppermute x3, starting transfers between devices, local(): lax.ppermute(compact, 'segment', [(i, (i + step) % sections) for i in ran...  5.97 us
    pallas_call x2, Pallas kernels, local(): pl.pallas_call(functools.partial(weight_kernel, sizes), out_shape=fl(2, c...  4.26 us
    ppermute x6, starting transfers between devices, partner(): lax.ppermute(array, axis, [(i, i ^ mask) for i in range(lax.axis_size(axi...  3.86 us
  transfers between devices with their start and end apart: 9, of which 7 were waited for; matrix products, arithmetic and copies ran while one was open for 3% of the time, Pallas kernels for 5%

profile of v2, /device:TPU:0, one launch (start us, length us, event | category | flops | bytes accessed | tf_op | source)
XLA Modules:
  0.0 149.4 jit_solution(4158014047668569987)
XLA Ops:
  0.7 1.4 copy.16
  2.5 1.6 %rev.4 = bf16[2,3,3,3,32,32]{5,2,4,3,1,0:T(4,128)(2,1)S(1)} reverse(bf16[2,3,3,3,32,32]{5,2,4,3,1,0:T(4,128)(2,1)S(1)} %copy.16), dimensions={1,2,3} | reverse | bytes 221184 | tf_op jit(solution)/shard_map/jit(_flip)/rev | solution.py:282
  4.8 3.0 %collective-permute-start = (bf16[2,2,9,32,128]{4,3,2,0,1:T(8,128)(2,1)S(1)}, bf16[2,2,9,32,128]{4,3,2,0,1:T(8,128)(2,1)S(1)}, u32[]{:S(2)}, u32[]{:S(2)}) collective-permute-start(bf16[2,2,9,32,128]{4,3,2,0,1:T(8,128)(2,1)S(1)} %get-tuple-element.139), channel_id=1, source_target_pairs={{0,8},{8,16},{16,24},{24,0},{1,9},{9,17},{17,25},{25,1},{2,10},{10... | collective-permute-start | bytes 884744 | tf_op jit(solution)/shard_map/ppermute | solution.py:288
  7.8 1.5 %collective-permute-start.1 = (bf16[2,2,9,32,128]{4,3,2,0,1:T(8,128)(2,1)S(1)}, bf16[2,2,9,32,128]{4,3,2,0,1:T(8,128)(2,1)S(1)}, u32[]{:S(2)}, u32[]{:S(2)}) collective-permute-start(bf16[2,2,9,32,128]{4,3,2,0,1:T(8,128)(2,1)S(1)} %get-tuple-element.139), channel_id=1, source_target_pairs={{0,16},{8,24},{16,0},{24,8},{1,17},{9,25},{17,1},{25,9},{2,18},{10... | collective-permute-start | bytes 884744 | tf_op jit(solution)/shard_map/ppermute | solution.py:288
  9.3 1.4 collective-permute-start.2
  11.5 7.8 %shard_map.58 = (bf16[4,64,128]{2,1,0:T(8,128)(2,1)}, bf16[4,64,128]{2,1,0:T(8,128)(2,1)}) custom-call(bf16[4,128,128]{2,1,0:T(8,128)(2,1)} %bitcast.91), custom_call_target="tpu_custom_call" | custom-call | tf_op jit(solution)/shard_map/pallas_call | solution.py:249
  20.1 2.0 %collective-permute-done.1 = bf16[2,2,9,32,128]{4,3,2,0,1:T(8,128)(2,1)S(1)} collective-permute-done((bf16[2,2,9,32,128]{4,3,2,0,1:T(8,128)(2,1)S(1)}, bf16[2,2,9,32,128]{4,3,2,0,1:T(8,128)(2,1)S(1)}, u32[]{:S(2)}, u32[]{:S(2)}) %collective-permute-start.1) | collective-permute-done | bytes 294944 | tf_op jit(solution)/shard_map/ppermute | solution.py:288
  23.8 1.7 %shard_map.59 = (bf16[4,128,128]{2,1,0:T(8,128)(2,1)S(1)}, bf16[4,128,128]{2,1,0:T(8,128)(2,1)S(1)}, bf16[4,256,128]{2,1,0:T(8,128)(2,1)S(1)}, bf16[4,256,128]{2...) custom-call(bf16[4,64,128]{2,1,0:T(8,128)(2,1)S(1)} %copy-done.49, ...), custom_call_target="tpu_custom_call" | custom-call | tf_op jit(solution)/shard_map/pallas_call | solution.py:317
  26.9 7.9 %shard_map.60 = (bf16[4,64,128]{2,1,0:T(8,128)(2,1)}, bf16[4,64,128]{2,1,0:T(8,128)(2,1)}) custom-call(bf16[4,128,128]{2,1,0:T(8,128)(2,1)} %copy-done.15), custom_call_target="tpu_custom_call" | custom-call | tf_op jit(solution)/shard_map/pallas_call | solution.py:249
  37.4 1.7 %shard_map.61 = (bf16[4,128,128]{2,1,0:T(8,128)(2,1)S(1)}, bf16[4,128,128]{2,1,0:T(8,128)(2,1)S(1)}, bf16[4,256,128]{2,1,0:T(8,128)(2,1)S(1)}, bf16[4,256,128]{2...) custom-call(bf16[4,64,128]{2,1,0:T(8,128)(2,1)S(1)} %copy-done.55, ...), custom_call_target="tpu_custom_call" | custom-call | tf_op jit(solution)/shard_map/pallas_call | solution.py:317
  41.9 7.4 %shard_map.62 = (bf16[4,64,128]{2,1,0:T(8,128)(2,1)}, bf16[4,64,128]{2,1,0:T(8,128)(2,1)}) custom-call(bf16[4,128,128]{2,1,0:T(8,128)(2,1)} %copy-done.13), custom_call_target="tpu_custom_call" | custom-call | tf_op jit(solution)/shard_map/pallas_call | solution.py:249
  51.9 1.7 %shard_map.63 = (bf16[4,128,128]{2,1,0:T(8,128)(2,1)S(1)}, bf16[4,128,128]{2,1,0:T(8,128)(2,1)S(1)}, bf16[4,256,128]{2,1,0:T(8,128)(2,1)S(1)}, bf16[4,256,128]{2...) custom-call(bf16[4,64,128]{2,1,0:T(8,128)(2,1)S(1)} %copy-done.53, ...), custom_call_target="tpu_custom_call" | custom-call | tf_op jit(solution)/shard_map/pallas_call | solution.py:317
  57.0 7.1 %shard_map.64 = (bf16[4,64,128]{2,1,0:T(8,128)(2,1)}, bf16[4,64,128]{2,1,0:T(8,128)(2,1)}) custom-call(bf16[4,128,128]{2,1,0:T(8,128)(2,1)} %copy-done.11), custom_call_target="tpu_custom_call" | custom-call | tf_op jit(solution)/shard_map/pallas_call | solution.py:249
  66.7 2.3 %shard_map.65 = (bf16[4,128,128]{2,1,0:T(8,128)(2,1)S(1)}, bf16[4,128,128]{2,1,0:T(8,128)(2,1)}, bf16[4,256,128]{2,1,0:T(8,128)(2,1)S(1)}, bf16[4,256,128]{2,1,0...) custom-call(bf16[4,64,128]{2,1,0:T(8,128)(2,1)S(1)} %copy-done.57, ...), custom_call_target="tpu_custom_call" | custom-call | tf_op jit(solution)/shard_map/pallas_call | solution.py:317
  70.5 1.7 %fusion.3.block_ref.mid_ref = bf16[4,128,128]{2,1,0:T(8,128)(2,1)} fusion(f32[4,128,128]{2,1,0:T(8,128)S(1)} %get-tuple-element.70, f32[4,4,32,128]{3,2,1,0:T(8,128)} %copy.23), kind=kLoop, calls=%fused_computation.13 | loop fusion | flops 131072 | bytes 655360 | tf_op jit(solution)/shard_map/convert_element_type | solution.py:339
  72.1 7.1 %shard_map.66 = (bf16[4,64,128]{2,1,0:T(8,128)(2,1)}, bf16[4,64,128]{2,1,0:T(8,128)(2,1)}) custom-call(bf16[4,128,128]{2,1,0:T(8,128)(2,1)} %fusion.3.block_ref.mid_ref), custom_call_target="tpu_custom_call" | custom-call | tf_op jit(solution)/shard_map/pallas_call | solution.py:249
  82.8 1.5 shard_map.67
  84.9 7.1 %shard_map.68 = (bf16[4,64,128]{2,1,0:T(8,128)(2,1)}, bf16[4,64,128]{2,1,0:T(8,128)(2,1)}) custom-call(bf16[4,128,128]{2,1,0:T(8,128)(2,1)} %copy-done.8), custom_call_target="tpu_custom_call" | custom-call | tf_op jit(solution)/shard_map/pallas_call | solution.py:249
  95.6 1.5 shard_map.69
  97.7 7.1 %shard_map.70 = (bf16[4,64,128]{2,1,0:T(8,128)(2,1)}, bf16[4,64,128]{2,1,0:T(8,128)(2,1)}) custom-call(bf16[4,128,128]{2,1,0:T(8,128)(2,1)} %copy-done.6), custom_call_target="tpu_custom_call" | custom-call | tf_op jit(solution)/shard_map/pallas_call | solution.py:249
  109.3 1.5 %shard_map.71 = (bf16[4,128,128]{2,1,0:T(8,128)(2,1)S(1)}, bf16[4,128,128]{2,1,0:T(8,128)(2,1)S(1)}, bf16[4,128,128]{2,1,0:T(8,128)(2,1)S(1)}) custom-call(bf16[4,64,128]{2,1,0:T(8,128)(2,1)S(1)} %copy-done.51, bf16[4,128,128]{2,1,0:T(8,128)(2,1)S(1)} %copy-done.7, bf16[4,64,128]{2,1,0:T(8,128)(2,1)S(1)} %copy-done.52, ...), custom_call_target="tpu_custom_call" | custom-call | tf_op jit(solution)/shard_map/pallas_call | solution.py:356
  112.8 7.1 %shard_map.72 = (bf16[4,64,128]{2,1,0:T(8,128)(2,1)}, bf16[4,64,128]{2,1,0:T(8,128)(2,1)}) custom-call(bf16[4,128,128]{2,1,0:T(8,128)(2,1)} %copy-done.4), custom_call_target="tpu_custom_call" | custom-call | tf_op jit(solution)/shard_map/pallas_call | solution.py:249
  121.1 1.7 %shard_map.73 = (bf16[4,128,128]{2,1,0:T(8,128)(2,1)S(1)}, bf16[4,128,128]{2,1,0:T(8,128)(2,1)S(1)}) custom-call(bf16[4,64,128]{2,1,0:T(8,128)(2,1)S(1)} %copy-done.47, bf16[4,128,128]{2,1,0:T(8,128)(2,1)S(1)} %copy-done.5, bf16[4,64,128]{2,1,0:T(8,128)(2,1)S(1)} %copy-done.48, bf16[9,32,128]{2,1,0:T(8,128)(2,1)S(1)} %get-tuple-element.123.first_ref, ...), custom_call_target="tpu_custom_call" | custom-call | tf_op jit(solution)/shard_map/pallas_call | solution.py:356
  122.8 2.1 %shard_map.75 = f32[2,32,864]{2,1,0:T(8,128)S(1)} custom-call(bf16[4,256,128]{2,1,0:T(8,128)(2,1)S(1)} %broadcast_select_fusion.1.frame_ref, bf16[4,128,128]{2,1,0:T(8,128)(2,1)S(1)} %broadcast_select_fusion.7.first_ref, bf16[4,256,128]{2,1,0:T(8,128)(2,1)S(1)} %broadcast_select_fusion.hidden_ref, bf16[4,128,128]{2,1,0:T(8,128)(2,1)S(1)} %broadcast_select_fusion.6.second_ref), custom_call_target="tpu_custom_call" | custom-call | tf_op jit(solution)/shard_map/pallas_call | solution.py:386
  125.0 2.1 %shard_map.74 = f32[2,32,864]{2,1,0:T(8,128)S(1)} custom-call(bf16[4,256,128]{2,1,0:T(8,128)(2,1)S(1)} %broadcast_select_fusion.3.frame_ref, bf16[4,128,128]{2,1,0:T(8,128)(2,1)S(1)} %broadcast_select_fusion.9.first_ref, bf16[4,256,128]{2,1,0:T(8,128)(2,1)S(1)} %broadcast_select_fusion.2.hidden_ref, bf16[4,128,128]{2,1,0:T(8,128)(2,1)S(1)} %broadcast_select_fusion.8.second_ref), custom_call_target="tpu_custom_call" | custom-call | tf_op jit(solution)/shard_map/pallas_call | solution.py:386
  127.2 1.5 %collective-permute-start.4 = (bf16[2,32,864]{2,1,0:T(8,128)(2,1)S(1)}, bf16[2,32,864]{2,1,0:T(8,128)(2,1)S(1)}, u32[]{:S(2)}, u32[]{:S(2)}) collective-permute-start(bf16[2,32,864]{2,1,0:T(8,128)(2,1)S(1)} %select_convert_fusion), channel_id=1, source_target_pairs={{0,8},{8,0},{16,24},{24,16},{1,9},{9,1},{17,25},{25,17},{2,10},{10... | collective-permute-start | bytes 331784 | tf_op jit(solution)/shard_map/ppermute | solution.py:261
  129.4 1.5 %collective-permute-start.3 = (bf16[4,128,128]{2,1,0:T(8,128)(2,1)S(1)}, bf16[4,128,128]{2,1,0:T(8,128)(2,1)S(1)}, u32[]{:S(2)}, u32[]{:S(2)}) collective-permute-start(bf16[4,128,128]{2,1,0:T(8,128)(2,1)S(1)} %get-tuple-element.111), channel_id=1, source_target_pairs={{0,8},{8,0},{16,24},{24,16},{1,9},{9,1},{17,25},{25,17},{2,10},{10... | collective-permute-start | bytes 393224 | tf_op jit(solution)/shard_map/ppermute | solution.py:261
  130.9 2.1 %collective-permute-done.4 = bf16[2,32,864]{2,1,0:T(8,128)(2,1)S(1)} collective-permute-done((bf16[2,32,864]{2,1,0:T(8,128)(2,1)S(1)}, bf16[2,32,864]{2,1,0:T(8,128)(2,1)S(1)}, u32[]{:S(2)}, u32[]{:S(2)}) %collective-permute-start.4) | collective-permute-done | bytes 110624 | tf_op jit(solution)/shard_map/ppermute | solution.py:261
  134.4 1.4 collective-permute-done.3
  137.2 3.8 %collective-permute-done.6 = bf16[2,32,864]{2,1,0:T(8,128)(2,1)S(1)} collective-permute-done((bf16[2,32,864]{2,1,0:T(8,128)(2,1)S(1)}, bf16[2,32,864]{2,1,0:T(8,128)(2,1)S(1)}, u32[]{:S(2)}, u32[]{:S(2)}) %collective-permute-start.6) | collective-permute-done | bytes 110624 | tf_op jit(solution)/shard_map/ppermute | solution.py:261
  142.1 5.5 %collective-permute-done.7 = bf16[2,32,864]{2,1,0:T(8,128)(2,1)S(1)} collective-permute-done((bf16[2,32,864]{2,1,0:T(8,128)(2,1)S(1)}, bf16[2,32,864]{2,1,0:T(8,128)(2,1)S(1)}, u32[]{:S(2)}, u32[]{:S(2)}) %collective-permute-start.7) | collective-permute-done | bytes 110624 | tf_op jit(solution)/shard_map/ppermute | solution.py:261
  148.0 1.4 copy.26
  (178 shorter events, 41.8 us)
Async XLA Ops:
  0.6 10.1 %copy-start = (bf16[2,32,4,4,128]{4,3,2,1,0:T(4,128)(2,1)S(1)}, bf16[2,32,4,4,128]{4,3,2,1,0:T(4,128)(2,1)}, u32[]{:S(2)}) copy-start(bf16[2,32,4,4,128]{4,3,2,1,0:T(4,128)(2,1)} %param.3) | copy-start | bytes 786436
  0.6 1.4 copy-start.63
  4.4 14.9 %copy-start.64 = (bf16[2,32,4,4,128]{4,3,2,1,0:T(4,128)(2,1)S(1)}, bf16[2,32,4,4,128]{4,3,2,1,0:T(4,128)(2,1)}, u32[]{:S(2)}) copy-start(bf16[2,32,4,4,128]{4,3,2,1,0:T(4,128)(2,1)} %param.4) | copy-start | bytes 786436
  4.8 15.3 %collective-permute-start = (bf16[2,2,9,32,128]{4,3,2,0,1:T(8,128)(2,1)S(1)}, bf16[2,2,9,32,128]{4,3,2,0,1:T(8,128)(2,1)S(1)}, u32[]{:S(2)}, u32[]{:S(2)}) collective-permute-start(bf16[2,2,9,32,128]{4,3,2,0,1:T(8,128)(2,1)S(1)} %get-tuple-element.139), channel_id=1, source_target_pairs={{0,8},{8,16},{16,24},{24,0},{1,9},{9,17},{17,25},{25,1},{2,10},{10... | collective-permute-start | bytes 884744 | tf_op jit(solution)/shard_map/ppermute | solution.py:288
  7.8 14.3 %collective-permute-start.1 = (bf16[2,2,9,32,128]{4,3,2,0,1:T(8,128)(2,1)S(1)}, bf16[2,2,9,32,128]{4,3,2,0,1:T(8,128)(2,1)S(1)}, u32[]{:S(2)}, u32[]{:S(2)}) collective-permute-start(bf16[2,2,9,32,128]{4,3,2,0,1:T(8,128)(2,1)S(1)} %get-tuple-element.139), channel_id=1, source_target_pairs={{0,16},{8,24},{16,0},{24,8},{1,17},{9,25},{17,1},{25,9},{2,18},{10... | collective-permute-start | bytes 884744 | tf_op jit(solution)/shard_map/ppermute | solution.py:288
  9.3 13.1 %collective-permute-start.2 = (bf16[2,2,9,32,128]{4,3,2,0,1:T(8,128)(2,1)S(1)}, bf16[2,2,9,32,128]{4,3,2,0,1:T(8,128)(2,1)S(1)}, u32[]{:S(2)}, u32[]{:S(2)}) collective-permute-start(bf16[2,2,9,32,128]{4,3,2,0,1:T(8,128)(2,1)S(1)} %get-tuple-element.139), channel_id=1, source_target_pairs={{0,24},{8,0},{16,8},{24,16},{1,25},{9,1},{17,9},{25,17},{2,26},{10... | collective-permute-start | bytes 884744 | tf_op jit(solution)/shard_map/ppermute | solution.py:288
  26.9 22.4 %copy-start.17 = (bf16[4,256,128]{2,1,0:T(8,128)(2,1)}, bf16[4,256,128]{2,1,0:T(8,128)(2,1)S(1)}, u32[]{:S(2)}) copy-start(bf16[4,256,128]{2,1,0:T(8,128)(2,1)S(1)} %get-tuple-element.94) | copy-start | bytes 786436
  41.9 7.4 %copy-start.39 = (bf16[4,128,128]{2,1,0:T(8,128)(2,1)}, bf16[4,128,128]{2,1,0:T(8,128)(2,1)S(1)}, u32[]{:S(2)}) copy-start(bf16[4,128,128]{2,1,0:T(8,128)(2,1)S(1)} %get-tuple-element.67) | copy-start | bytes 393220
  70.5 8.8 %copy-start.43 = (bf16[4,128,128]{2,1,0:T(8,128)(2,1)}, bf16[4,128,128]{2,1,0:T(8,128)(2,1)S(1)}, u32[]{:S(2)}) copy-start(bf16[4,128,128]{2,1,0:T(8,128)(2,1)S(1)} %get-tuple-element.66) | copy-start | bytes 393220
  82.8 22.1 %copy-start.3 = (bf16[4,128,128]{2,1,0:T(8,128)(2,1)S(1)}, bf16[4,128,128]{2,1,0:T(8,128)(2,1)}, u32[]{:S(2)}) copy-start(bf16[4,128,128]{2,1,0:T(8,128)(2,1)} %fusion.3.block_ref.mid_ref) | copy-start | bytes 393220
  84.9 7.1 %copy-start.35 = (bf16[4,128,128]{2,1,0:T(8,128)(2,1)}, bf16[4,128,128]{2,1,0:T(8,128)(2,1)S(1)}, u32[]{:S(2)}) copy-start(bf16[4,128,128]{2,1,0:T(8,128)(2,1)S(1)} %get-tuple-element.97) | copy-start | bytes 393220
  95.6 16.6 %copy-start.10 = (bf16[4,128,128]{2,1,0:T(8,128)(2,1)S(1)}, bf16[4,128,128]{2,1,0:T(8,128)(2,1)}, u32[]{:S(2)}) copy-start(bf16[4,128,128]{2,1,0:T(8,128)(2,1)} %copy-done.8) | copy-start | bytes 393220
  97.7 22.1 %copy-start.18 = (bf16[4,256,128]{2,1,0:T(8,128)(2,1)S(1)}, bf16[4,256,128]{2,1,0:T(8,128)(2,1)}, u32[]{:S(2)}) copy-start(bf16[4,256,128]{2,1,0:T(8,128)(2,1)} %copy-done.17) | copy-start | bytes 786436
  109.3 10.6 %copy-start.26 = (bf16[4,256,128]{2,1,0:T(8,128)(2,1)S(1)}, bf16[4,256,128]{2,1,0:T(8,128)(2,1)}, u32[]{:S(2)}) copy-start(bf16[4,256,128]{2,1,0:T(8,128)(2,1)} %copy-done.25) | copy-start | bytes 786436
  112.2 7.9 %copy-start.24 = (bf16[4,256,128]{2,1,0:T(8,128)(2,1)S(1)}, bf16[4,256,128]{2,1,0:T(8,128)(2,1)}, u32[]{:S(2)}) copy-start(bf16[4,256,128]{2,1,0:T(8,128)(2,1)} %copy-done.23) | copy-start | bytes 786436
  119.9 1.0 copy-start.20
  119.9 1.0 copy-start.29
  120.0 1.0 copy-start.36
  120.0 1.0 copy-start.38
  120.0 1.0 copy-start.5
  120.0 1.0 copy-start.47
  120.1 1.0 copy-start.48
  122.8 5.9 %copy-start.46 = (bf16[4,128,128]{2,1,0:T(8,128)(2,1)S(1)}, bf16[4,128,128]{2,1,0:T(8,128)(2,1)}, u32[]{:S(2)}) copy-start(bf16[4,128,128]{2,1,0:T(8,128)(2,1)} %copy-done.45) | copy-start | bytes 393220
  124.9 4.4 %copy-start.40 = (bf16[4,128,128]{2,1,0:T(8,128)(2,1)S(1)}, bf16[4,128,128]{2,1,0:T(8,128)(2,1)}, u32[]{:S(2)}) copy-start(bf16[4,128,128]{2,1,0:T(8,128)(2,1)} %copy-done.39) | copy-start | bytes 393220
  124.9 4.4 %copy-start.42 = (bf16[4,128,128]{2,1,0:T(8,128)(2,1)S(1)}, bf16[4,128,128]{2,1,0:T(8,128)(2,1)}, u32[]{:S(2)}) copy-start(bf16[4,128,128]{2,1,0:T(8,128)(2,1)} %copy-done.41) | copy-start | bytes 393220
  125.0 4.4 %copy-start.44 = (bf16[4,128,128]{2,1,0:T(8,128)(2,1)S(1)}, bf16[4,128,128]{2,1,0:T(8,128)(2,1)}, u32[]{:S(2)}) copy-start(bf16[4,128,128]{2,1,0:T(8,128)(2,1)} %copy-done.43) | copy-start | bytes 393220
  127.2 5.8 %collective-permute-start.4 = (bf16[2,32,864]{2,1,0:T(8,128)(2,1)S(1)}, bf16[2,32,864]{2,1,0:T(8,128)(2,1)S(1)}, u32[]{:S(2)}, u32[]{:S(2)}) collective-permute-start(bf16[2,32,864]{2,1,0:T(8,128)(2,1)S(1)} %select_convert_fusion), channel_id=1, source_target_pairs={{0,8},{8,0},{16,24},{24,16},{1,9},{9,1},{17,25},{25,17},{2,10},{10... | collective-permute-start | bytes 331784 | tf_op jit(solution)/shard_map/ppermute | solution.py:261
  128.7 5.7 %collective-permute-start.8 = (bf16[4,128,128]{2,1,0:T(8,128)(2,1)S(1)}, bf16[4,128,128]{2,1,0:T(8,128)(2,1)S(1)}, u32[]{:S(2)}, u32[]{:S(2)}) collective-permute-start(bf16[4,128,128]{2,1,0:T(8,128)(2,1)S(1)} %get-tuple-element.106), channel_id=1, source_target_pairs={{0,8},{8,0},{16,24},{24,16},{1,9},{9,1},{17,25},{25,17},{2,10},{10... | collective-permute-start | bytes 393224 | tf_op jit(solution)/shard_map/ppermute | solution.py:261
  129.4 6.4 %collective-permute-start.3 = (bf16[4,128,128]{2,1,0:T(8,128)(2,1)S(1)}, bf16[4,128,128]{2,1,0:T(8,128)(2,1)S(1)}, u32[]{:S(2)}, u32[]{:S(2)}) collective-permute-start(bf16[4,128,128]{2,1,0:T(8,128)(2,1)S(1)} %get-tuple-element.111), channel_id=1, source_target_pairs={{0,8},{8,0},{16,24},{24,16},{1,9},{9,1},{17,25},{25,17},{2,10},{10... | collective-permute-start | bytes 393224 | tf_op jit(solution)/shard_map/ppermute | solution.py:261
  133.1 3.1 %collective-permute-start.5 = (bf16[2,32,864]{2,1,0:T(8,128)(2,1)S(1)}, bf16[2,32,864]{2,1,0:T(8,128)(2,1)S(1)}, u32[]{:S(2)}, u32[]{:S(2)}) collective-permute-start(bf16[2,32,864]{2,1,0:T(8,128)(2,1)S(1)} %get-tuple-element.109), channel_id=1, source_target_pairs={{0,1},{1,0},{2,3},{3,2},{4,5},{5,4},{6,7},{7,6},{8,9},{9,8},{10,11... | collective-permute-start | bytes 331784 | tf_op jit(solution)/shard_map/ppermute | solution.py:261
  136.2 4.9 %collective-permute-start.6 = (bf16[2,32,864]{2,1,0:T(8,128)(2,1)S(1)}, bf16[2,32,864]{2,1,0:T(8,128)(2,1)S(1)}, u32[]{:S(2)}, u32[]{:S(2)}) collective-permute-start(bf16[2,32,864]{2,1,0:T(8,128)(2,1)S(1)} %fusion.4), channel_id=1, source_target_pairs={{0,2},{1,3},{2,0},{3,1},{4,6},{5,7},{6,4},{7,5},{8,10},{9,11},{10,... | collective-permute-start | bytes 331784 | tf_op jit(solution)/shard_map/ppermute | solution.py:261
  141.1 6.4 %collective-permute-start.7 = (bf16[2,32,864]{2,1,0:T(8,128)(2,1)S(1)}, bf16[2,32,864]{2,1,0:T(8,128)(2,1)S(1)}, u32[]{:S(2)}, u32[]{:S(2)}) collective-permute-start(bf16[2,32,864]{2,1,0:T(8,128)(2,1)S(1)} %fusion.5), channel_id=1, source_target_pairs={{0,4},{1,5},{2,6},{3,7},{4,0},{5,1},{6,2},{7,3},{8,12},{9,13},{10,... | collective-permute-start | bytes 331784 | tf_op jit(solution)/shard_map/ppermute | solution.py:261
  (42 other events, 33.3 us)
